TPU v7x, 32 devices: a whole 2x2x4 slice. The times are simulated.
32 devices in a mesh: sub: 8 (over z, y), grp: 4 (over x, core).
Axes of the slice: x: 2, y: 2, z: 4, core: 2. Of those that a mesh axis runs over, the one named last changes fastest.
Arguments:
- interior_factor: bfloat16 [32, 2048, 2048], P(('sub', 'grp')), may hold values from -0.25 to 2, as said below
- interface_coupling: bfloat16 [32, 2048, 512], P(('sub', 'grp')), may hold values from -0.09375 to 0.09375
- interface_block: float32 [32, 512, 512], P(('sub', 'grp')), may hold values from -0.5 to 4, as said below
- sample_panel: bfloat16 [4096, 128], P('sub'), may hold values from -6 to 6
- index_map: int32 [32, 4], P(('sub', 'grp')), may hold values from 0 to 31, as said below
- block_count: int32 [32], P(('sub', 'grp')), may hold values from 1 to 4
Outputs:
- sampled: float32 [4096, 128], P(('sub', 'grp'))
Inputs may be any that keep to these rules, and one draw needn't show every extreme that they name: `index_map`: local block a of subdomain s is global block o * 4 + a, where o is s // 4, or one more or one less than it modulo 32 // 4. `interior_factor`: each matrix is lower triangular with its diagonal in 1 to 2. `interface_block`: each matrix is symmetric with its diagonal in 2 to 4.
All inputs are finite; a program needn't handle non-finite values.
Results may differ from a plain program's by a relative error of at most 0.0012.
Values sent between devices are 32-bit elements; how exact they have to be, the bound alone decides.
No kernel may reach another device: no remote copies, remote signals or barrier semaphores. Data moves between devices by JAX's collectives and lax.ppermute only.
A program may use at most 64 MiB of HBM per device.

v0:
```python
import jax
import jax.numpy as jnp
from jax import lax
from jax.sharding import PartitionSpec as P

POWER = 3


def passed_along(block, axis, distance):
    devices = range(lax.axis_size(axis))
    route = [((i - distance) % len(devices), i) for i in devices]
    return lax.ppermute(block, axis, route)


def spread_rows(block):
    return lax.all_gather(block, "grp", axis=0, tiled=True)


def local(
    interior_factor, interface_coupling, interface_block, sample_panel, index_map, block_count
):
    factor = interior_factor[0]
    coupling = interface_coupling[0]
    coupled = jnp.dot(factor, coupling, preferred_element_type=jnp.float32).astype(jnp.bfloat16)
    gram = lax.dot_general(
        coupled, coupled, (((0,), (0,)), ((), ())), preferred_element_type=jnp.float32
    )
    schur = interface_block[0] - gram
    ids = index_map[0]
    count = block_count[0]
    nblk = ids.shape[0]
    width = schur.shape[0]
    blk = width // nblk
    samples = sample_panel.shape[1]
    cycles = lax.axis_size("sub")
    groups = lax.axis_size("grp")
    home = lax.axis_index("sub")
    live = (jnp.arange(nblk, dtype=jnp.int32) < count).astype(jnp.float32)
    masked = (
        schur.reshape(nblk, blk, nblk, blk) * live[:, None, None, None] * live[None, None, :, None]
    )
    owners = ids // groups
    dest = (owners - home + cycles + 1) % cycles - 1
    current = sample_panel.astype(jnp.float32)
    column = (dest + 1) * groups + ids % groups
    frame = jnp.arange(3 * groups, dtype=jnp.int32)
    selector = (column[:, None] == frame[None, :]).astype(jnp.float32)
    flat = masked.reshape(width, width)
    result = None
    for step in range(POWER):
        pieces = []
        for offset in (-1, 0, 1):
            if offset == 0:
                pieces.append(current)
            else:
                pieces.append(passed_along(current, "sub", -offset))
        near = jnp.concatenate(pieces, axis=0).reshape(3 * groups, blk, samples)
        picked = jnp.einsum("bq,qcn->bcn", selector, near, precision=lax.Precision.HIGHEST)
        product = jnp.dot(flat, picked.reshape(width, samples), precision=lax.Precision.HIGHEST)
        product = product.reshape(nblk, blk, samples)
        got_terms, got_dest = (
            lax.all_to_all(product, "grp", split_axis=0, concat_axis=0, tiled=True),
            lax.all_to_all(
                dest.astype(jnp.float32), "grp", split_axis=0, concat_axis=0, tiled=True
            ),
        )
        total = jnp.sum(got_terms * (got_dest == 0).astype(jnp.float32)[:, None, None], axis=0)
        for offset in (-1, 1):
            keep = (got_dest == offset).astype(jnp.float32)[:, None, None]
            summed = jnp.sum(got_terms * keep, axis=0)
            total = total + passed_along(summed, "sub", offset)
        result = 0.5 * total
        if step + 1 < POWER:
            current = spread_rows(result)
    return result


def solution(mesh):
    return jax.shard_map(
        local,
        mesh=mesh,
        in_specs=(
            P(("sub", "grp"), None, None),
            P(("sub", "grp"), None, None),
            P(("sub", "grp"), None, None),
            P("sub", None),
            P(("sub", "grp"), None),
            P(("sub", "grp")),
        ),
        out_specs=P(("sub", "grp"), None),
        check_vma=False,
    )
```

profile of v0, /device:TPU:0, one launch (start us, length us, event | category | flops | bytes accessed | tf_op | source)
XLA Modules:
  0.0 129.2 jit_solution(14007389528576588260)
XLA Ops:
  1.1 6.1 %collective-permute-start.1 = (f32[512,128]{1,0:T(8,128)S(1)}, f32[512,128]{1,0:T(8,128)}, u32[]{:S(2)}, u32[]{:S(2)}) collective-permute-start(f32[512,128]{1,0:T(8,128)S(1)} %convert_element_type.44), channel_id=1, source_target_pairs={{4,0},{8,4},{12,8},{16,12},{20,16},{24,20},{28,24},{0,28},{5,1},{9... | collective-permute-start | bytes 786440 | tf_op jit(solution)/shard_map/ppermute | solution.py:12
  8.5 3.2 %all-to-all-start.1 = ((f32[4,1,1]{2,1,0:T(1,128)}), f32[4,1,1]{2,1,0:T(1,128)S(1)}, u32[]{:S(2)}, u32[]{:S(2)}) async-start(f32[4,1,1]{2,1,0:T(1,128)} %copy.22), calls=%async_computation.1 | async-start | bytes 4096 | tf_op jit(solution)/shard_map/all_to_all | solution.py:63
  12.5 16.0 %fusion.7 = f32[512,512]{1,0:T(8,128)S(1)} fusion(bf16[1,2048,2048]{2,1,0:T(8,128)(2,1)} %param.6, bf16[1,2048,512]{2,1,0:T(8,128)(2,1)S(1)} %copy-done, f32[1,512,512]{2,1,0:T(8,128)} %param.8, f32[512]{0:T(512)S(1)} %broadcast_bitcast_fusion), kind=kOutput, calls=%fused_computation.6 | convolution fusion | flops 5370544128 | bytes 12584960 | tf_op jit(solution)/shard_map/dot_general | solution.py:25
  28.5 1.1 pad_maximum_fusion
  30.5 1.7 %fusion.31 = f32[4,128,128]{2,1,0:T(8,128)} fusion(f32[4,128,512]{2,1,0:T(8,128)S(1)} %bitcast.65, f32[512,128,1]{1,0,2:T(8,128)S(1)} %bitcast.72), kind=kOutput, calls=%fused_computation.61 | convolution fusion | flops 402653184 | bytes 1572864 | tf_op jit(solution)/shard_map/dot_general | solution.py:59
  32.2 3.4 %all-to-all-start = ((f32[4,128,128]{2,1,0:T(8,128)}), f32[4,128,128]{2,1,0:T(8,128)S(1)}, u32[]{:S(2)}, u32[]{:S(2)}) async-start(f32[4,128,128]{2,1,0:T(8,128)} %fusion.31), calls=%async_computation | async-start | bytes 524288 | tf_op jit(solution)/shard_map/all_to_all | solution.py:62
  35.8 5.9 %all-to-all-done = f32[4,128,128]{2,1,0:T(8,128)S(1)} async-done(((f32[4,128,128]{2,1,0:T(8,128)}), f32[4,128,128]{2,1,0:T(8,128)S(1)}, u32[]{:S(2)}, u32[]{:S(2)}) %all-to-all-start) | async-done | bytes 262176 | tf_op jit(solution)/shard_map/all_to_all | solution.py:62
  41.7 4.8 %collective-permute-start.2 = (f32[128,128]{1,0:T(8,128)S(1)}, f32[128,128]{1,0:T(8,128)S(1)}, u32[]{:S(2)}, u32[]{:S(2)}) collective-permute-start(f32[128,128]{1,0:T(8,128)S(1)} %get-tuple-element.11), channel_id=1, source_target_pairs={{4,0},{8,4},{12,8},{16,12},{20,16},{24,20},{28,24},{0,28},{5,1},{9... | collective-permute-start | bytes 196616 | tf_op jit(solution)/shard_map/ppermute | solution.py:12
  46.5 1.9 %collective-permute-done.2 = f32[128,128]{1,0:T(8,128)S(1)} collective-permute-done((f32[128,128]{1,0:T(8,128)S(1)}, f32[128,128]{1,0:T(8,128)S(1)}, u32[]{:S(2)}, u32[]{:S(2)}) %collective-permute-start.2) | collective-permute-done | bytes 65568 | tf_op jit(solution)/shard_map/ppermute | solution.py:12
  48.4 5.1 %collective-permute-done.3 = f32[128,128]{1,0:T(8,128)S(1)} collective-permute-done((f32[128,128]{1,0:T(8,128)S(1)}, f32[128,128]{1,0:T(8,128)S(1)}, u32[]{:S(2)}, u32[]{:S(2)}) %collective-permute-start.3) | collective-permute-done | bytes 65568 | tf_op jit(solution)/shard_map/ppermute | solution.py:12
  53.5 5.8 %all_gather.6 = f32[512,128]{1,0:T(8,128)S(1)} all-gather(f32[128,128]{1,0:T(8,128)S(1)} %add_multiply_fusion.2), channel_id=1, replica_groups=mesh['sub'=8,'grp'=4] {'grp'}, dimensions={0}, use_global_device_ids=true | all-gather | bytes 327680 | tf_op jit(solution)/shard_map/all_gather | solution.py:16
  59.3 2.0 %collective-permute-start.4 = (f32[512,128]{1,0:T(8,128)S(1)}, f32[512,128]{1,0:T(8,128)S(1)}, u32[]{:S(2)}, u32[]{:S(2)}) collective-permute-start(f32[512,128]{1,0:T(8,128)S(1)} %all_gather.6), channel_id=1, source_target_pairs={{28,0},{0,4},{4,8},{8,12},{12,16},{16,20},{20,24},{24,28},{29,1},{... | collective-permute-start | bytes 786440 | tf_op jit(solution)/shard_map/ppermute | solution.py:12
  61.3 12.1 %collective-permute-done.5 = f32[512,128]{1,0:T(8,128)S(1)} collective-permute-done((f32[512,128]{1,0:T(8,128)S(1)}, f32[512,128]{1,0:T(8,128)S(1)}, u32[]{:S(2)}, u32[]{:S(2)}) %collective-permute-start.5) | collective-permute-done | bytes 262176 | tf_op jit(solution)/shard_map/ppermute | solution.py:12
  75.4 8.4 %all_to_all.23 = f32[4,128,128]{2,1,0:T(8,128)S(1)} all-to-all(f32[4,128,128]{2,1,0:T(8,128)S(1)} %fusion.32), channel_id=1, replica_groups=mesh['sub'=8,'grp'=4] {'grp'}, dimensions={0} | all-to-all | bytes 524288 | tf_op jit(solution)/shard_map/all_to_all | solution.py:62
  84.0 2.0 %collective-permute-start.7 = (f32[128,128]{1,0:T(8,128)S(1)}, f32[128,128]{1,0:T(8,128)S(1)}, u32[]{:S(2)}, u32[]{:S(2)}) collective-permute-start(f32[128,128]{1,0:T(8,128)S(1)} %get-tuple-element.9), channel_id=1, source_target_pairs={{28,0},{0,4},{4,8},{8,12},{12,16},{16,20},{20,24},{24,28},{29,1},{... | collective-permute-start | bytes 196616 | tf_op jit(solution)/shard_map/ppermute | solution.py:12
  86.0 2.2 %collective-permute-done.6 = f32[128,128]{1,0:T(8,128)S(1)} collective-permute-done((f32[128,128]{1,0:T(8,128)S(1)}, f32[128,128]{1,0:T(8,128)S(1)}, u32[]{:S(2)}, u32[]{:S(2)}) %collective-permute-start.6) | collective-permute-done | bytes 65568 | tf_op jit(solution)/shard_map/ppermute | solution.py:12
  88.3 2.8 %collective-permute-done.7 = f32[128,128]{1,0:T(8,128)S(1)} collective-permute-done((f32[128,128]{1,0:T(8,128)S(1)}, f32[128,128]{1,0:T(8,128)S(1)}, u32[]{:S(2)}, u32[]{:S(2)}) %collective-permute-start.7) | collective-permute-done | bytes 65568 | tf_op jit(solution)/shard_map/ppermute | solution.py:12
  91.0 5.8 %all_gather.7 = f32[512,128]{1,0:T(8,128)S(1)} all-gather(f32[128,128]{1,0:T(8,128)S(1)} %add_multiply_fusion.1), channel_id=1, replica_groups=mesh['sub'=8,'grp'=4] {'grp'}, dimensions={0}, use_global_device_ids=true | all-gather | bytes 327680 | tf_op jit(solution)/shard_map/all_gather | solution.py:16
  96.8 2.0 %collective-permute-start.8 = (f32[512,128]{1,0:T(8,128)S(1)}, f32[512,128]{1,0:T(8,128)S(1)}, u32[]{:S(2)}, u32[]{:S(2)}) collective-permute-start(f32[512,128]{1,0:T(8,128)S(1)} %all_gather.7), channel_id=1, source_target_pairs={{28,0},{0,4},{4,8},{8,12},{12,16},{16,20},{20,24},{24,28},{29,1},{... | collective-permute-start | bytes 786440 | tf_op jit(solution)/shard_map/ppermute | solution.py:12
  98.8 12.1 %collective-permute-done.9 = f32[512,128]{1,0:T(8,128)S(1)} collective-permute-done((f32[512,128]{1,0:T(8,128)S(1)}, f32[512,128]{1,0:T(8,128)S(1)}, u32[]{:S(2)}, u32[]{:S(2)}) %collective-permute-start.9) | collective-permute-done | bytes 262176 | tf_op jit(solution)/shard_map/ppermute | solution.py:12
  113.0 8.4 %all_to_all.24 = f32[4,128,128]{2,1,0:T(8,128)S(1)} all-to-all(f32[4,128,128]{2,1,0:T(8,128)S(1)} %fusion.33), channel_id=1, replica_groups=mesh['sub'=8,'grp'=4] {'grp'}, dimensions={0} | all-to-all | bytes 524288 | tf_op jit(solution)/shard_map/all_to_all | solution.py:62
  121.6 2.0 %collective-permute-start.11 = (f32[128,128]{1,0:T(8,128)S(1)}, f32[128,128]{1,0:T(8,128)S(1)}, u32[]{:S(2)}, u32[]{:S(2)}) collective-permute-start(f32[128,128]{1,0:T(8,128)S(1)} %get-tuple-element.6), channel_id=1, source_target_pairs={{28,0},{0,4},{4,8},{8,12},{12,16},{16,20},{20,24},{24,28},{29,1},{... | collective-permute-start | bytes 196616 | tf_op jit(solution)/shard_map/ppermute | solution.py:12
  123.6 2.2 %collective-permute-done.10 = f32[128,128]{1,0:T(8,128)S(1)} collective-permute-done((f32[128,128]{1,0:T(8,128)S(1)}, f32[128,128]{1,0:T(8,128)S(1)}, u32[]{:S(2)}, u32[]{:S(2)}) %collective-permute-start.10) | collective-permute-done | bytes 65568 | tf_op jit(solution)/shard_map/ppermute | solution.py:12
  125.8 2.8 %collective-permute-done.11 = f32[128,128]{1,0:T(8,128)S(1)} collective-permute-done((f32[128,128]{1,0:T(8,128)S(1)}, f32[128,128]{1,0:T(8,128)S(1)}, u32[]{:S(2)}, u32[]{:S(2)}) %collective-permute-start.11) | collective-permute-done | bytes 65568 | tf_op jit(solution)/shard_map/ppermute | solution.py:12
  (38 shorter events, 8.6 us)
Async XLA Ops:
  0.0 12.5 %copy-start = (bf16[1,2048,512]{2,1,0:T(8,128)(2,1)S(1)}, bf16[1,2048,512]{2,1,0:T(8,128)(2,1)}, u32[]{:S(2)}) copy-start(bf16[1,2048,512]{2,1,0:T(8,128)(2,1)} %param.7) | copy-start | bytes 6291460
  1.1 27.4 %collective-permute-start.1 = (f32[512,128]{1,0:T(8,128)S(1)}, f32[512,128]{1,0:T(8,128)}, u32[]{:S(2)}, u32[]{:S(2)}) collective-permute-start(f32[512,128]{1,0:T(8,128)S(1)} %convert_element_type.44), channel_id=1, source_target_pairs={{4,0},{8,4},{12,8},{16,12},{20,16},{24,20},{28,24},{0,28},{5,1},{9... | collective-permute-start | bytes 786440 | tf_op jit(solution)/shard_map/ppermute | solution.py:12
  7.2 21.3 %collective-permute-start = (f32[512,128]{1,0:T(8,128)S(1)}, f32[512,128]{1,0:T(8,128)}, u32[]{:S(2)}, u32[]{:S(2)}) collective-permute-start(f32[512,128]{1,0:T(8,128)S(1)} %convert_element_type.44), channel_id=1, source_target_pairs={{28,0},{0,4},{4,8},{8,12},{12,16},{16,20},{20,24},{24,28},{29,1},{... | collective-permute-start | bytes 786440 | tf_op jit(solution)/shard_map/ppermute | solution.py:12
  8.5 23.7 %all-to-all-start.1 = ((f32[4,1,1]{2,1,0:T(1,128)}), f32[4,1,1]{2,1,0:T(1,128)S(1)}, u32[]{:S(2)}, u32[]{:S(2)}) async-start(f32[4,1,1]{2,1,0:T(1,128)} %copy.22), calls=%async_computation.1 | async-start | bytes 4096 | tf_op jit(solution)/shard_map/all_to_all | solution.py:63
  12.5 16.0 %copy-start.1 = (s32[1,4]{1,0:T(1,128)S(1)}, s32[1,4]{1,0:T(1,128)}, u32[]{:S(2)}) copy-start(s32[1,4]{1,0:T(1,128)} %param.10) | copy-start | bytes 52
  32.2 9.4 %all-to-all-start = ((f32[4,128,128]{2,1,0:T(8,128)}), f32[4,128,128]{2,1,0:T(8,128)S(1)}, u32[]{:S(2)}, u32[]{:S(2)}) async-start(f32[4,128,128]{2,1,0:T(8,128)} %fusion.31), calls=%async_computation | async-start | bytes 524288 | tf_op jit(solution)/shard_map/all_to_all | solution.py:62
  41.7 6.7 %collective-permute-start.2 = (f32[128,128]{1,0:T(8,128)S(1)}, f32[128,128]{1,0:T(8,128)S(1)}, u32[]{:S(2)}, u32[]{:S(2)}) collective-permute-start(f32[128,128]{1,0:T(8,128)S(1)} %get-tuple-element.11), channel_id=1, source_target_pairs={{4,0},{8,4},{12,8},{16,12},{20,16},{24,20},{28,24},{0,28},{5,1},{9... | collective-permute-start | bytes 196616 | tf_op jit(solution)/shard_map/ppermute | solution.py:12
  46.5 7.0 %collective-permute-start.3 = (f32[128,128]{1,0:T(8,128)S(1)}, f32[128,128]{1,0:T(8,128)S(1)}, u32[]{:S(2)}, u32[]{:S(2)}) collective-permute-start(f32[128,128]{1,0:T(8,128)S(1)} %get-tuple-element.12), channel_id=1, source_target_pairs={{28,0},{0,4},{4,8},{8,12},{12,16},{16,20},{20,24},{24,28},{29,1},{... | collective-permute-start | bytes 196616 | tf_op jit(solution)/shard_map/ppermute | solution.py:12
  59.3 14.2 %collective-permute-start.5 = (f32[512,128]{1,0:T(8,128)S(1)}, f32[512,128]{1,0:T(8,128)S(1)}, u32[]{:S(2)}, u32[]{:S(2)}) collective-permute-start(f32[512,128]{1,0:T(8,128)S(1)} %all_gather.6), channel_id=1, source_target_pairs={{4,0},{8,4},{12,8},{16,12},{20,16},{24,20},{28,24},{0,28},{5,1},{9... | collective-permute-start | bytes 786440 | tf_op jit(solution)/shard_map/ppermute | solution.py:12
  59.3 14.2 %collective-permute-start.4 = (f32[512,128]{1,0:T(8,128)S(1)}, f32[512,128]{1,0:T(8,128)S(1)}, u32[]{:S(2)}, u32[]{:S(2)}) collective-permute-start(f32[512,128]{1,0:T(8,128)S(1)} %all_gather.6), channel_id=1, source_target_pairs={{28,0},{0,4},{4,8},{8,12},{12,16},{16,20},{20,24},{24,28},{29,1},{... | collective-permute-start | bytes 786440 | tf_op jit(solution)/shard_map/ppermute | solution.py:12
  83.9 4.3 %collective-permute-start.6 = (f32[128,128]{1,0:T(8,128)S(1)}, f32[128,128]{1,0:T(8,128)S(1)}, u32[]{:S(2)}, u32[]{:S(2)}) collective-permute-start(f32[128,128]{1,0:T(8,128)S(1)} %get-tuple-element.8), channel_id=1, source_target_pairs={{4,0},{8,4},{12,8},{16,12},{20,16},{24,20},{28,24},{0,28},{5,1},{9... | collective-permute-start | bytes 196616 | tf_op jit(solution)/shard_map/ppermute | solution.py:12
  84.0 7.0 %collective-permute-start.7 = (f32[128,128]{1,0:T(8,128)S(1)}, f32[128,128]{1,0:T(8,128)S(1)}, u32[]{:S(2)}, u32[]{:S(2)}) collective-permute-start(f32[128,128]{1,0:T(8,128)S(1)} %get-tuple-element.9), channel_id=1, source_target_pairs={{28,0},{0,4},{4,8},{8,12},{12,16},{16,20},{20,24},{24,28},{29,1},{... | collective-permute-start | bytes 196616 | tf_op jit(solution)/shard_map/ppermute | solution.py:12
  96.8 14.2 %collective-permute-start.9 = (f32[512,128]{1,0:T(8,128)S(1)}, f32[512,128]{1,0:T(8,128)S(1)}, u32[]{:S(2)}, u32[]{:S(2)}) collective-permute-start(f32[512,128]{1,0:T(8,128)S(1)} %all_gather.7), channel_id=1, source_target_pairs={{4,0},{8,4},{12,8},{16,12},{20,16},{24,20},{28,24},{0,28},{5,1},{9... | collective-permute-start | bytes 786440 | tf_op jit(solution)/shard_map/ppermute | solution.py:12
  96.8 14.2 %collective-permute-start.8 = (f32[512,128]{1,0:T(8,128)S(1)}, f32[512,128]{1,0:T(8,128)S(1)}, u32[]{:S(2)}, u32[]{:S(2)}) collective-permute-start(f32[512,128]{1,0:T(8,128)S(1)} %all_gather.7), channel_id=1, source_target_pairs={{28,0},{0,4},{4,8},{8,12},{12,16},{16,20},{20,24},{24,28},{29,1},{... | collective-permute-start | bytes 786440 | tf_op jit(solution)/shard_map/ppermute | solution.py:12
  121.5 4.3 %collective-permute-start.10 = (f32[128,128]{1,0:T(8,128)S(1)}, f32[128,128]{1,0:T(8,128)S(1)}, u32[]{:S(2)}, u32[]{:S(2)}) collective-permute-start(f32[128,128]{1,0:T(8,128)S(1)} %get-tuple-element.5), channel_id=1, source_target_pairs={{4,0},{8,4},{12,8},{16,12},{20,16},{24,20},{28,24},{0,28},{5,1},{9... | collective-permute-start | bytes 196616 | tf_op jit(solution)/shard_map/ppermute | solution.py:12
  121.6 7.0 %collective-permute-start.11 = (f32[128,128]{1,0:T(8,128)S(1)}, f32[128,128]{1,0:T(8,128)S(1)}, u32[]{:S(2)}, u32[]{:S(2)}) collective-permute-start(f32[128,128]{1,0:T(8,128)S(1)} %get-tuple-element.6), channel_id=1, source_target_pairs={{28,0},{0,4},{4,8},{8,12},{12,16},{16,20},{20,24},{24,28},{29,1},{... | collective-permute-start | bytes 196616 | tf_op jit(solution)/shard_map/ppermute | solution.py:12
where the time goes:
time: 130 us; the launch traced here: 129 us
  waiting for transfers between devices  47.1 us (36%)
  blocking collectives  28.3 us (22%)
  starting transfers between devices  25.7 us (20%)
  matrix products  22.3 us (17%)
  other arithmetic  4.09 us (3%)
    ppermute x12, waiting for transfers between devices, passed_along(): return lax.ppermute(block, axis, route)  41.3 us
    ppermute x12, starting transfers between devices, passed_along(): return lax.ppermute(block, axis, route)  19.1 us
    all_to_all x2, blocking collectives, local(): lax.all_to_all(product, 'grp', split_axis=0, concat_axis=0, tiled=True)  16.8 us
    dot_general x1, matrix products, local(): lax.dot_general(coupled, coupled, (((0,), (0,)), ((), ())), preferred_ele...  16 us
    all_gather x2, blocking collectives, spread_rows(): return lax.all_gather(block, 'grp', axis=0, tiled=True)  11.6 us
    all_to_all x1, waiting for transfers between devices, local(): lax.all_to_all(product, 'grp', split_axis=0, concat_axis=0, tiled=True)  5.85 us
    dot_general x3, matrix products, local(): jnp.dot(flat, picked.reshape(width, samples), precision=lax.Precision.HIG...  3.66 us
    all_to_all x1, starting transfers between devices, local(): lax.all_to_all(product, 'grp', split_axis=0, concat_axis=0, tiled=True)  3.41 us
  transfers between devices with their start and end apart: 14, of which 9 were waited for; matrix products, arithmetic and copies ran while one was open for 16% of the time, Pallas kernels for 0%

commit v1 on v0

v1 whole, which is shorter than its diff:
```python
import jax
import jax.numpy as jnp
from jax import lax
from jax.experimental import pallas as pl
from jax.experimental.pallas import tpu as pltpu
from jax.sharding import PartitionSpec as P

POWER = 3
TILE = 256
TAIL = 8


def sub_shift(block, distance):
    size = lax.axis_size("sub")
    return lax.ppermute(block, "sub", [(i, (i + distance) % size) for i in range(size)])


def grp_shift(block, distance):
    size = lax.axis_size("grp")
    return lax.ppermute(block, "grp", [(i, (i + distance) % size) for i in range(size)])


def schur_kernel(info, factor, coupling, block, high, low, fbuf, cbuf, bbuf, coupled, fsem, csem, bsem):
    ni, width = coupling.shape
    nblk = info.shape[0] - 2
    blk = width // nblk
    steps = ni // TILE
    rows = [pl.ds(i * TILE, TILE) for i in range(steps)]
    loads = []
    for i in range(steps):
        ccopy = pltpu.make_async_copy(coupling.at[rows[i]], cbuf.at[rows[i]], csem.at[i])
        span = pl.ds(0, (i + 1) * TILE)
        fcopy = pltpu.make_async_copy(factor.at[rows[i], span], fbuf.at[rows[i], span], fsem.at[i])
        ccopy.start()
        fcopy.start()
        loads.append((ccopy, fcopy))
    bcopy = pltpu.make_async_copy(block, bbuf, bsem)
    bcopy.start()
    for i in range(steps):
        for copy in loads[i]:
            copy.wait()
        span = (i + 1) * TILE
        part = jnp.dot(
            fbuf[rows[i], 0:span], cbuf[0:span, :], preferred_element_type=jnp.float32
        )
        coupled[rows[i], :] = part.astype(jnp.bfloat16)
    gram = lax.dot_general(
        coupled[...], coupled[...], (((0,), (0,)), ((), ())), preferred_element_type=jnp.float32
    )
    bcopy.wait()
    member = info[0]
    count = info[1]
    for a in range(nblk):
        row = pl.multiple_of(lax.rem(a - member + nblk, nblk) * blk, blk)
        for b in range(nblk):
            col = pl.multiple_of(lax.rem(member - b + nblk, nblk) * blk, blk)
            cut = (slice(a * blk, (a + 1) * blk), slice(b * blk, (b + 1) * blk))
            scale = jnp.where(max(a, b) < count, 0.5, 0.0).astype(jnp.float32)
            value = (bbuf[cut] - gram[cut]) * scale
            top = value.astype(jnp.bfloat16)
            high[pl.ds(row, blk), pl.ds(col, blk)] = top
            low[pl.ds(row, blk), pl.ds(col, blk)] = (value - top.astype(jnp.float32)).astype(
                jnp.bfloat16
            )


def first_kernel(info, high, low, own, near, far, *terms):
    nblk = len(terms)
    blk = own.shape[0] // nblk
    member = info[0]
    even = lax.rem(member, 2) == 0
    picked = []
    for r in range(nblk):
        b = lax.rem(member - r + nblk, nblk)
        span = pl.ds(pl.multiple_of(b * blk, blk), blk)
        dest = info[2 + b]
        use_near = jnp.logical_or(
            jnp.logical_and(dest == -1, even), jnp.logical_and(dest == 1, jnp.logical_not(even))
        )
        other = jnp.where(use_near, near[span, :], far[span, :])
        picked.append(jnp.where(dest == 0, own[span, :], other))
    vector = jnp.concatenate(picked, axis=0).astype(jnp.bfloat16)
    product = jnp.dot(high[...], vector, preferred_element_type=jnp.float32)
    product = product + jnp.dot(low[...], vector, preferred_element_type=jnp.float32)
    for r in range(nblk):
        terms[r][0:blk, :] = product[r * blk : (r + 1) * blk, :]
        dest = info[2 + lax.rem(member + r, nblk)]
        terms[r][blk : blk + TAIL, :] = jnp.full(
            (TAIL, own.shape[1]), dest.astype(jnp.float32), jnp.float32
        )


def apply_kernel(high, low, *refs):
    nblk = len(refs) // 2
    blk = refs[0].shape[0]
    vector = jnp.concatenate([ref[...] for ref in refs[:nblk]], axis=0)
    top = vector.astype(jnp.bfloat16)
    rest = (vector - top.astype(jnp.float32)).astype(jnp.bfloat16)
    product = jnp.dot(high[...], top, preferred_element_type=jnp.float32)
    product = product + jnp.dot(high[...], rest, preferred_element_type=jnp.float32)
    product = product + jnp.dot(low[...], top, preferred_element_type=jnp.float32)
    for r in range(nblk):
        refs[nblk + r][...] = product[r * blk : (r + 1) * blk, :]


def local(
    interior_factor, interface_coupling, interface_block, sample_panel, index_map, block_count
):
    factor = interior_factor[0]
    coupling = interface_coupling[0]
    block = interface_block[0]
    ids = index_map[0]
    nblk = ids.shape[0]
    ni, width = coupling.shape
    blk = width // nblk
    samples = sample_panel.shape[1]
    cycles = lax.axis_size("sub")
    groups = lax.axis_size("grp")
    home = lax.axis_index("sub")
    member = lax.axis_index("grp").astype(jnp.int32)
    dest = (ids // groups - home + cycles + 1) % cycles - 1
    info = jnp.concatenate([member[None], block_count, dest]).astype(jnp.int32)
    smem = pl.BlockSpec(memory_space=pltpu.SMEM)
    anywhere = pl.BlockSpec(memory_space=pl.ANY)
    vmem = pl.BlockSpec(memory_space=pltpu.VMEM)

    own = sample_panel.astype(jnp.float32)
    route = []
    for o in range(cycles):
        for g in range(groups):
            step = 1 if g % 2 == 0 else -1
            route.append((o * groups + g, ((o + step) % cycles) * groups + g))
    near = lax.ppermute(own, ("sub", "grp"), route)

    steps = ni // TILE
    half = jax.ShapeDtypeStruct((width, width), jnp.bfloat16)
    high, low = pl.pallas_call(
        schur_kernel,
        out_shape=(half, half),
        in_specs=[smem, anywhere, anywhere, anywhere],
        out_specs=(vmem, vmem),
        scratch_shapes=[
            pltpu.VMEM((ni, ni), jnp.bfloat16),
            pltpu.VMEM((ni, width), jnp.bfloat16),
            pltpu.VMEM((width, width), jnp.float32),
            pltpu.VMEM((ni, width), jnp.bfloat16),
            pltpu.SemaphoreType.DMA((steps,)),
            pltpu.SemaphoreType.DMA((steps,)),
            pltpu.SemaphoreType.DMA,
        ],
        cost_estimate=pl.CostEstimate(
            flops=ni * ni * width + 2 * ni * width * width,
            bytes_accessed=ni * ni + 2 * ni * width + 4 * width * width,
            transcendentals=0,
        ),
        compiler_params=pltpu.CompilerParams(vmem_limit_bytes=32 * 1024 * 1024),
        name="schur",
    )(info, factor, coupling, block)

    far = lax.ppermute(near, "grp", [(g, g ^ 1) for g in range(groups)])
    tall = jax.ShapeDtypeStruct((blk + TAIL, samples), jnp.float32)
    short = jax.ShapeDtypeStruct((blk, samples), jnp.float32)
    terms = pl.pallas_call(
        first_kernel,
        out_shape=(tall,) * nblk,
        in_specs=[smem] + [vmem] * 5,
        out_specs=(vmem,) * nblk,
        name="first",
    )(info, high, low, own, near, far)

    owners = None
    for step in range(POWER):
        if step > 0:
            terms = pl.pallas_call(
                apply_kernel,
                out_shape=(short,) * nblk,
                in_specs=[vmem] * (2 + nblk),
                out_specs=(vmem,) * nblk,
                name="apply",
            )(high, low, *picked)
        got = [terms[0]] + [grp_shift(terms[r], r) for r in range(1, groups)]
        if step == 0:
            owners = [g[blk : blk + 1, :] for g in got]
            got = [g[:blk] for g in got]
        zero = jnp.zeros((blk, samples), jnp.float32)
        sums = {}
        for d in (-1, 0, 1):
            sums[d] = sum(jnp.where(owners[r] == d, got[r], zero) for r in range(groups))
        if step + 1 < POWER:
            behind = sub_shift(jnp.concatenate([sums[0], sums[1]]), 1)
            ahead = sub_shift(jnp.concatenate([sums[0], sums[-1]]), -1)
            behind2 = sub_shift(sums[1], 2)
            ahead2 = sub_shift(sums[-1], -2)
            here = sums[0] + behind[blk:] + ahead[blk:]
            after = ahead[:blk] + sums[1] + ahead2
            before = behind[:blk] + sums[-1] + behind2
            picked = []
            for r in range(groups):
                owner = owners[(groups - r) % groups]
                chosen = jnp.where(owner == 0, here, jnp.where(owner == 1, after, before))
                picked.append(chosen if r == 0 else grp_shift(chosen, r))
    return sums[0] + sub_shift(sums[1], 1) + sub_shift(sums[-1], -1)


def solution(mesh):
    return jax.shard_map(
        local,
        mesh=mesh,
        in_specs=(
            P(("sub", "grp"), None, None),
            P(("sub", "grp"), None, None),
            P(("sub", "grp"), None, None),
            P("sub", None),
            P(("sub", "grp"), None),
            P(("sub", "grp")),
        ),
        out_specs=P(("sub", "grp"), None),
        check_vma=False,
    )
```

time: 130 us -> 103 us (0.79)
  blocking collectives: 28.3 us -> 0 us
  matrix products: 22.3 us -> 0 us
  Pallas kernels: 0 us -> 13.9 us
  waiting for transfers between devices: 47.1 us -> 37.2 us
  local copies, waits for them, and re-layouts: 0.8 us -> 9.88 us
  starting transfers between devices: 25.7 us -> 31.9 us
  other arithmetic: 4.09 us -> 8.83 us
    dot_general x7 -> x0, matrix products: 22.3 us -> none  [the longest x1 16 us: local(): lax.dot_general(coupled, coupled, (((0,), (0,)), ((), ())), preferred_ele...]
    all_to_all x2 -> x0, blocking collectives: 16.8 us -> none  [local(): lax.all_to_all(product, 'grp', split_axis=0, concat_axis=0, tiled=True)]
    pallas_call x0 -> x4, Pallas kernels: none -> 13.9 us  [the longest x1 6.56 us: local(): pl.pallas_call(schur_kernel, out_shape=(half, half), in_specs=[smem, anyw...]
    ppermute x12 -> x27, starting transfers between devices: 19.1 us -> 31.9 us  [the longest x10 18.1 us: sub_shift(): lax.ppermute(block, 'sub', [(i, (i + distance) % size) for i in range(siz...]
    all_gather x2 -> x0, blocking collectives: 11.6 us -> none  [spread_rows(): return lax.all_gather(block, 'grp', axis=0, tiled=True)]
    unnamed x4 -> x30, local copies, waits for them, and re-layouts: 0.01 us -> 9.88 us
    all_to_all x2 -> x0, starting transfers between devices: 6.63 us -> none  [the longest x1 3.41 us: local(): lax.all_to_all(product, 'grp', split_axis=0, concat_axis=0, tiled=True)]
    all_to_all x2 -> x0, waiting for transfers between devices: 5.86 us -> none  [the longest x1 5.85 us: local(): lax.all_to_all(product, 'grp', split_axis=0, concat_axis=0, tiled=True)]
  transfers between devices with their start and end apart: 14 -> 27, of which waited for: 9 -> 19; matrix products, arithmetic and copies ran while one was open for 16% -> 3% of each run, Pallas kernels for 0% -> 6%
where the time goes in v1:
time: 103 us
  waiting for transfers between devices  37.2 us (36%)
  starting transfers between devices  31.9 us (31%)
  Pallas kernels  13.9 us (13%)
  local copies, waits for them, and re-layouts  9.88 us (10%)
  other arithmetic  8.83 us (9%)
    ppermute x10, starting transfers between devices, sub_shift(): lax.ppermute(block, 'sub', [(i, (i + distance) % size) for i in range(siz...  18.1 us
    ppermute x10, waiting for transfers between devices, sub_shift(): lax.ppermute(block, 'sub', [(i, (i + distance) % size) for i in range(siz...  15.7 us
    ppermute x15, waiting for transfers between devices, grp_shift(): lax.ppermute(block, 'grp', [(i, (i + distance) % size) for i in range(siz...  15.5 us
    ppermute x15, starting transfers between devices, grp_shift(): lax.ppermute(block, 'grp', [(i, (i + distance) % size) for i in range(siz...  10.7 us
    unnamed x30, local copies, waits for them, and re-layouts  9.88 us
    pallas_call x1, Pallas kernels, local(): pl.pallas_call(schur_kernel, out_shape=(half, half), in_specs=[smem, anyw...  6.56 us
    ppermute x1, waiting for transfers between devices, local(): near = lax.ppermute(own, ('sub', 'grp'), route)  5.98 us
    pallas_call x2, Pallas kernels, local(): pl.pallas_call(apply_kernel, out_shape=(short,) * nblk, in_specs=[vmem] *...  4.85 us
  transfers between devices with their start and end apart: 27, of which 19 were waited for; matrix products, arithmetic and copies ran while one was open for 3% of the time, Pallas kernels for 6%

profile of v1, /device:TPU:0, one launch (start us, length us, event | category | flops | bytes accessed | tf_op | source)
XLA Modules:
  0.0 102.5 jit_solution(18139421298118411536)
XLA Ops:
  0.9 3.0 %collective-permute-start = (f32[512,128]{1,0:T(8,128)S(1)}, f32[512,128]{1,0:T(8,128)S(1)}, u32[]{:S(2)}, u32[]{:S(2)}) collective-permute-start(f32[512,128]{1,0:T(8,128)S(1)} %convert_element_type.3.own), channel_id=1, source_target_pairs={{0,4},{1,29},{2,6},{3,31},{4,8},{5,1},{6,10},{7,3},{8,12},{9,5},{1... | collective-permute-start | bytes 786440 | tf_op jit(solution)/shard_map/ppermute | solution.py:133
  5.4 6.0 %collective-permute-done.near = f32[512,128]{1,0:T(8,128)S(1)} collective-permute-done((f32[512,128]{1,0:T(8,128)S(1)}, f32[512,128]{1,0:T(8,128)S(1)}, u32[]{:S(2)}, u32[]{:S(2)}) %collective-permute-start) | collective-permute-done | bytes 262176 | tf_op jit(solution)/shard_map/ppermute | solution.py:133
  11.4 3.5 %copy-done.3 = bf16[1,2048,2048]{2,1,0:T(8,128)(2,1)S(1)} copy-done((bf16[1,2048,2048]{2,1,0:T(8,128)(2,1)S(1)}, bf16[1,2048,2048]{2,1,0:T(8,128)(2,1)}, u32[]{:S(2)}) %copy-start.3) | copy-done | bytes 8388632
  14.9 1.6 %copy-done.4 = bf16[1,2048,512]{2,1,0:T(8,128)(2,1)S(1)} copy-done((bf16[1,2048,512]{2,1,0:T(8,128)(2,1)S(1)}, bf16[1,2048,512]{2,1,0:T(8,128)(2,1)}, u32[]{:S(2)}) %copy-start.4) | copy-done | bytes 2097176
  17.7 6.6 %schur.1 = (bf16[512,512]{1,0:T(8,128)(2,1)S(1)}, bf16[512,512]{1,0:T(8,128)(2,1)S(1)}) custom-call(s32[6]{0:T(128)S(1)} %pad_add_fusion.info, bf16[2048,2048]{1,0:T(8,128)(2,1)S(1)} %bitcast.38, bf16[2048,512]{1,0:T(8,128)(2,1)S(1)} %bitcast.39, f32[512,512]{1,0:T(8,128)S(1)} %bitcast.40), custom_call_target="tpu_custom_call" | custom-call | flops 3221225472 | bytes 7340032 | tf_op jit(solution)/shard_map/schur/pallas_call | solution.py:137
  26.6 2.5 %first.1 = (f32[136,128]{1,0:T(8,128)}, f32[136,128]{1,0:T(8,128)}, f32[136,128]{1,0:T(8,128)}, f32[136,128]{1,0:T(8,128)}) custom-call(s32[6]{0:T(128)} %copy-done.2, bf16[512,512]{1,0:T(8,128)(2,1)} %copy-done, bf16[512,512]{1,0:T(8,128)(2,1)} %copy-done.1, f32[512,128]{1,0:T(8,128)} %copy-done.6, f32[512,128]{1,0:T(8,128)} %copy-done.7, f32[512,128]{1,0:T(8,128)} %copy-done.8), custom_call_target="tpu_custom_call" | custom-call | tf_op jit(solution)/shard_map/first/pallas_call | solution.py:163
  30.2 1.7 %collective-permute-start.3 = (f32[136,128]{1,0:T(8,128)}, f32[136,128]{1,0:T(8,128)S(1)}, u32[]{:S(2)}, u32[]{:S(2)}) collective-permute-start(f32[136,128]{1,0:T(8,128)} %get-tuple-element.23), channel_id=1, source_target_pairs={{0,2},{1,3},{2,0},{3,1},{4,6},{5,7},{6,4},{7,5},{8,10},{9,11},{10,... | collective-permute-start | bytes 208904 | tf_op jit(solution)/shard_map/ppermute | solution.py:20
  33.1 2.0 %collective-permute-done.3 = f32[136,128]{1,0:T(8,128)S(1)} collective-permute-done((f32[136,128]{1,0:T(8,128)}, f32[136,128]{1,0:T(8,128)S(1)}, u32[]{:S(2)}, u32[]{:S(2)}) %collective-permute-start.3) | collective-permute-done | bytes 69664 | tf_op jit(solution)/shard_map/ppermute | solution.py:20
  37.0 5.0 %collective-permute-start.6 = (f32[256,128]{1,0:T(8,128)S(1)}, f32[256,128]{1,0:T(8,128)S(1)}, u32[]{:S(2)}, u32[]{:S(2)}) collective-permute-start(f32[256,128]{1,0:T(8,128)S(1)} %get-tuple-element.68), channel_id=1, source_target_pairs={{0,28},{4,0},{8,4},{12,8},{16,12},{20,16},{24,20},{28,24},{1,29},{... | collective-permute-start | bytes 393224 | tf_op jit(solution)/shard_map/ppermute | solution.py:15
  41.9 3.8 %collective-permute-start.7 = (f32[128,128]{1,0:T(8,128)S(1)}, f32[128,128]{1,0:T(8,128)S(1)}, u32[]{:S(2)}, u32[]{:S(2)}) collective-permute-start(f32[128,128]{1,0:T(8,128)S(1)} %select_add_fusion.5), channel_id=1, source_target_pairs={{0,24},{4,28},{8,0},{12,4},{16,8},{20,12},{24,16},{28,20},{1,25},{... | collective-permute-start | bytes 196616 | tf_op jit(solution)/shard_map/ppermute | solution.py:15
  45.8 2.9 %collective-permute-done.8 = f32[128,128]{1,0:T(8,128)S(1)} collective-permute-done((f32[128,128]{1,0:T(8,128)S(1)}, f32[128,128]{1,0:T(8,128)S(1)}, u32[]{:S(2)}, u32[]{:S(2)}) %collective-permute-start.8) | collective-permute-done | bytes 65568 | tf_op jit(solution)/shard_map/ppermute | solution.py:15
  48.7 2.4 %collective-permute-done.5 = f32[256,128]{1,0:T(8,128)S(1)} collective-permute-done((f32[256,128]{1,0:T(8,128)S(1)}, f32[256,128]{1,0:T(8,128)S(1)}, u32[]{:S(2)}, u32[]{:S(2)}) %collective-permute-start.5) | collective-permute-done | bytes 131104 | tf_op jit(solution)/shard_map/ppermute | solution.py:15
  53.1 3.7 %collective-permute-done.10.refs_2_ = f32[128,128]{1,0:T(8,128)S(1)} collective-permute-done((f32[128,128]{1,0:T(8,128)S(1)}, f32[128,128]{1,0:T(8,128)S(1)}, u32[]{:S(2)}, u32[]{:S(2)}) %collective-permute-start.10) | collective-permute-done | bytes 65568 | tf_op jit(solution)/shard_map/ppermute | solution.py:20
  57.7 2.4 %apply.2 = (f32[128,128]{1,0:T(8,128)}, f32[128,128]{1,0:T(8,128)}, f32[128,128]{1,0:T(8,128)}, f32[128,128]{1,0:T(8,128)}) custom-call(bf16[512,512]{1,0:T(8,128)(2,1)} %copy-done, bf16[512,512]{1,0:T(8,128)(2,1)} %copy-done.1, f32[128,128]{1,0:T(8,128)} %get-tuple-element.53.refs_0_, f32[128,128]{1,0:T(8,128)} %copy-done.14, f32[128,128]{1,0:T(8,128)} %copy-done.12, ...), custom_call_target="tpu_custom_call" | custom-call | tf_op jit(solution)/shard_map/apply/pallas_call | solution.py:174
  62.6 1.5 %collective-permute-done.12 = f32[128,128]{1,0:T(8,128)S(1)} collective-permute-done((f32[128,128]{1,0:T(8,128)}, f32[128,128]{1,0:T(8,128)S(1)}, u32[]{:S(2)}, u32[]{:S(2)}) %collective-permute-start.12) | collective-permute-done | bytes 65568 | tf_op jit(solution)/shard_map/ppermute | solution.py:20
  66.2 2.0 %collective-permute-start.16 = (f32[256,128]{1,0:T(8,128)S(1)}, f32[256,128]{1,0:T(8,128)S(1)}, u32[]{:S(2)}, u32[]{:S(2)}) collective-permute-start(f32[256,128]{1,0:T(8,128)S(1)} %get-tuple-element.66), channel_id=1, source_target_pairs={{0,28},{4,0},{8,4},{12,8},{16,12},{20,16},{24,20},{28,24},{1,29},{... | collective-permute-start | bytes 393224 | tf_op jit(solution)/shard_map/ppermute | solution.py:15
  68.3 2.4 %collective-permute-start.17 = (f32[128,128]{1,0:T(8,128)S(1)}, f32[128,128]{1,0:T(8,128)S(1)}, u32[]{:S(2)}, u32[]{:S(2)}) collective-permute-start(f32[128,128]{1,0:T(8,128)S(1)} %get-tuple-element.46), channel_id=1, source_target_pairs={{0,24},{4,28},{8,0},{12,4},{16,8},{20,12},{24,16},{28,20},{1,25},{... | collective-permute-start | bytes 196616 | tf_op jit(solution)/shard_map/ppermute | solution.py:15
  70.8 4.4 %collective-permute-done.17 = f32[128,128]{1,0:T(8,128)S(1)} collective-permute-done((f32[128,128]{1,0:T(8,128)S(1)}, f32[128,128]{1,0:T(8,128)S(1)}, u32[]{:S(2)}, u32[]{:S(2)}) %collective-permute-start.17) | collective-permute-done | bytes 65568 | tf_op jit(solution)/shard_map/ppermute | solution.py:15
  75.1 2.6 %collective-permute-done.18 = f32[128,128]{1,0:T(8,128)S(1)} collective-permute-done((f32[128,128]{1,0:T(8,128)S(1)}, f32[128,128]{1,0:T(8,128)S(1)}, u32[]{:S(2)}, u32[]{:S(2)}) %collective-permute-start.18) | collective-permute-done | bytes 65568 | tf_op jit(solution)/shard_map/ppermute | solution.py:15
  79.9 3.3 %collective-permute-done.20.refs_2_ = f32[128,128]{1,0:T(8,128)S(1)} collective-permute-done((f32[128,128]{1,0:T(8,128)S(1)}, f32[128,128]{1,0:T(8,128)S(1)}, u32[]{:S(2)}, u32[]{:S(2)}) %collective-permute-start.20) | collective-permute-done | bytes 65568 | tf_op jit(solution)/shard_map/ppermute | solution.py:20
  84.3 2.4 %apply.3 = (f32[128,128]{1,0:T(8,128)}, f32[128,128]{1,0:T(8,128)}, f32[128,128]{1,0:T(8,128)}, f32[128,128]{1,0:T(8,128)}) custom-call(bf16[512,512]{1,0:T(8,128)(2,1)} %copy-done, bf16[512,512]{1,0:T(8,128)(2,1)} %copy-done.1, f32[128,128]{1,0:T(8,128)} %get-tuple-element.50.refs_0_, f32[128,128]{1,0:T(8,128)} %copy-done.13, f32[128,128]{1,0:T(8,128)} %copy-done.11, ...), custom_call_target="tpu_custom_call" | custom-call | tf_op jit(solution)/shard_map/apply/pallas_call | solution.py:174
  92.8 2.5 %collective-permute-start.25 = (f32[128,128]{1,0:T(8,128)S(1)}, f32[128,128]{1,0:T(8,128)S(1)}, u32[]{:S(2)}, u32[]{:S(2)}) collective-permute-start(f32[128,128]{1,0:T(8,128)S(1)} %get-tuple-element.43), channel_id=1, source_target_pairs={{0,4},{4,8},{8,12},{12,16},{16,20},{20,24},{24,28},{28,0},{1,5},{5... | collective-permute-start | bytes 196616 | tf_op jit(solution)/shard_map/ppermute | solution.py:15
  95.3 2.3 %collective-permute-start.26 = (f32[128,128]{1,0:T(8,128)S(1)}, f32[128,128]{1,0:T(8,128)S(1)}, u32[]{:S(2)}, u32[]{:S(2)}) collective-permute-start(f32[128,128]{1,0:T(8,128)S(1)} %get-tuple-element.44), channel_id=1, source_target_pairs={{0,28},{4,0},{8,4},{12,8},{16,12},{20,16},{24,20},{28,24},{1,29},{... | collective-permute-start | bytes 196616 | tf_op jit(solution)/shard_map/ppermute | solution.py:15
  97.6 2.7 %collective-permute-done.25 = f32[128,128]{1,0:T(8,128)S(1)} collective-permute-done((f32[128,128]{1,0:T(8,128)S(1)}, f32[128,128]{1,0:T(8,128)S(1)}, u32[]{:S(2)}, u32[]{:S(2)}) %collective-permute-start.25) | collective-permute-done | bytes 65568 | tf_op jit(solution)/shard_map/ppermute | solution.py:15
  (82 shorter events, 28.5 us)
Async XLA Ops:
  0.9 10.4 %collective-permute-start = (f32[512,128]{1,0:T(8,128)S(1)}, f32[512,128]{1,0:T(8,128)S(1)}, u32[]{:S(2)}, u32[]{:S(2)}) collective-permute-start(f32[512,128]{1,0:T(8,128)S(1)} %convert_element_type.3.own), channel_id=1, source_target_pairs={{0,4},{1,29},{2,6},{3,31},{4,8},{5,1},{6,10},{7,3},{8,12},{9,5},{1... | collective-permute-start | bytes 786440 | tf_op jit(solution)/shard_map/ppermute | solution.py:133
  11.4 14.5 %collective-permute-start.1 = (f32[512,128]{1,0:T(8,128)S(1)}, f32[512,128]{1,0:T(8,128)S(1)}, u32[]{:S(2)}, u32[]{:S(2)}) collective-permute-start(f32[512,128]{1,0:T(8,128)S(1)} %collective-permute-done.near), channel_id=1, source_target_pairs={{0,1},{1,0},{2,3},{3,2},{4,5},{5,4},{6,7},{7,6},{8,9},{9,8},{10,11... | collective-permute-start | bytes 786440 | tf_op jit(solution)/shard_map/ppermute | solution.py:160
  29.1 3.9 %collective-permute-start.2 = (f32[136,128]{1,0:T(8,128)}, f32[136,128]{1,0:T(8,128)S(1)}, u32[]{:S(2)}, u32[]{:S(2)}) collective-permute-start(f32[136,128]{1,0:T(8,128)} %get-tuple-element.22), channel_id=1, source_target_pairs={{0,1},{1,2},{2,3},{3,0},{4,5},{5,6},{6,7},{7,4},{8,9},{9,10},{10,1... | collective-permute-start | bytes 208904 | tf_op jit(solution)/shard_map/ppermute | solution.py:20
  30.2 4.9 %collective-permute-start.3 = (f32[136,128]{1,0:T(8,128)}, f32[136,128]{1,0:T(8,128)S(1)}, u32[]{:S(2)}, u32[]{:S(2)}) collective-permute-start(f32[136,128]{1,0:T(8,128)} %get-tuple-element.23), channel_id=1, source_target_pairs={{0,2},{1,3},{2,0},{3,1},{4,6},{5,7},{6,4},{7,5},{8,10},{9,11},{10,... | collective-permute-start | bytes 208904 | tf_op jit(solution)/shard_map/ppermute | solution.py:20
  37.0 11.7 %collective-permute-start.6 = (f32[256,128]{1,0:T(8,128)S(1)}, f32[256,128]{1,0:T(8,128)S(1)}, u32[]{:S(2)}, u32[]{:S(2)}) collective-permute-start(f32[256,128]{1,0:T(8,128)S(1)} %get-tuple-element.68), channel_id=1, source_target_pairs={{0,28},{4,0},{8,4},{12,8},{16,12},{20,16},{24,20},{28,24},{1,29},{... | collective-permute-start | bytes 393224 | tf_op jit(solution)/shard_map/ppermute | solution.py:15
  41.9 9.2 %collective-permute-start.5 = (f32[256,128]{1,0:T(8,128)S(1)}, f32[256,128]{1,0:T(8,128)S(1)}, u32[]{:S(2)}, u32[]{:S(2)}) collective-permute-start(f32[256,128]{1,0:T(8,128)S(1)} %get-tuple-element.69), channel_id=1, source_target_pairs={{0,4},{4,8},{8,12},{12,16},{16,20},{20,24},{24,28},{28,0},{1,5},{5... | collective-permute-start | bytes 393224 | tf_op jit(solution)/shard_map/ppermute | solution.py:15
  41.9 6.8 %collective-permute-start.8 = (f32[128,128]{1,0:T(8,128)S(1)}, f32[128,128]{1,0:T(8,128)S(1)}, u32[]{:S(2)}, u32[]{:S(2)}) collective-permute-start(f32[128,128]{1,0:T(8,128)S(1)} %get-tuple-element.42), channel_id=1, source_target_pairs={{0,8},{4,12},{8,16},{12,20},{16,24},{20,28},{24,0},{28,4},{1,9},{5... | collective-permute-start | bytes 196616 | tf_op jit(solution)/shard_map/ppermute | solution.py:15
  41.9 6.8 %collective-permute-start.7 = (f32[128,128]{1,0:T(8,128)S(1)}, f32[128,128]{1,0:T(8,128)S(1)}, u32[]{:S(2)}, u32[]{:S(2)}) collective-permute-start(f32[128,128]{1,0:T(8,128)S(1)} %select_add_fusion.5), channel_id=1, source_target_pairs={{0,24},{4,28},{8,0},{12,4},{16,8},{20,12},{24,16},{28,20},{1,25},{... | collective-permute-start | bytes 196616 | tf_op jit(solution)/shard_map/ppermute | solution.py:15
  51.8 5.0 %collective-permute-start.10 = (f32[128,128]{1,0:T(8,128)S(1)}, f32[128,128]{1,0:T(8,128)S(1)}, u32[]{:S(2)}, u32[]{:S(2)}) collective-permute-start(f32[128,128]{1,0:T(8,128)S(1)} %get-tuple-element.51), channel_id=1, source_target_pairs={{0,2},{1,3},{2,0},{3,1},{4,6},{5,7},{6,4},{7,5},{8,10},{9,11},{10,... | collective-permute-start | bytes 196616 | tf_op jit(solution)/shard_map/ppermute | solution.py:20
  52.8 4.2 %collective-permute-start.9 = (f32[128,128]{1,0:T(8,128)S(1)}, f32[128,128]{1,0:T(8,128)S(1)}, u32[]{:S(2)}, u32[]{:S(2)}) collective-permute-start(f32[128,128]{1,0:T(8,128)S(1)} %get-tuple-element.52), channel_id=1, source_target_pairs={{0,1},{1,2},{2,3},{3,0},{4,5},{5,6},{6,7},{7,4},{8,9},{9,10},{10,1... | collective-permute-start | bytes 196616 | tf_op jit(solution)/shard_map/ppermute | solution.py:20
  60.1 4.0 %collective-permute-start.12 = (f32[128,128]{1,0:T(8,128)}, f32[128,128]{1,0:T(8,128)S(1)}, u32[]{:S(2)}, u32[]{:S(2)}) collective-permute-start(f32[128,128]{1,0:T(8,128)} %get-tuple-element.26), channel_id=1, source_target_pairs={{0,1},{1,2},{2,3},{3,0},{4,5},{5,6},{6,7},{7,4},{8,9},{9,10},{10,1... | collective-permute-start | bytes 196616 | tf_op jit(solution)/shard_map/ppermute | solution.py:20
  60.1 5.2 %collective-permute-start.13 = (f32[128,128]{1,0:T(8,128)}, f32[128,128]{1,0:T(8,128)S(1)}, u32[]{:S(2)}, u32[]{:S(2)}) collective-permute-start(f32[128,128]{1,0:T(8,128)} %get-tuple-element.27), channel_id=1, source_target_pairs={{0,2},{1,3},{2,0},{3,1},{4,6},{5,7},{6,4},{7,5},{8,10},{9,11},{10,... | collective-permute-start | bytes 196616 | tf_op jit(solution)/shard_map/ppermute | solution.py:20
  61.1 4.2 %collective-permute-start.14 = (f32[128,128]{1,0:T(8,128)}, f32[128,128]{1,0:T(8,128)S(1)}, u32[]{:S(2)}, u32[]{:S(2)}) collective-permute-start(f32[128,128]{1,0:T(8,128)} %get-tuple-element.28), channel_id=1, source_target_pairs={{0,3},{1,0},{2,1},{3,2},{4,7},{5,4},{6,5},{7,6},{8,11},{9,8},{10,9... | collective-permute-start | bytes 196616 | tf_op jit(solution)/shard_map/ppermute | solution.py:20
  66.2 11.5 %collective-permute-start.16 = (f32[256,128]{1,0:T(8,128)S(1)}, f32[256,128]{1,0:T(8,128)S(1)}, u32[]{:S(2)}, u32[]{:S(2)}) collective-permute-start(f32[256,128]{1,0:T(8,128)S(1)} %get-tuple-element.66), channel_id=1, source_target_pairs={{0,28},{4,0},{8,4},{12,8},{16,12},{20,16},{24,20},{28,24},{1,29},{... | collective-permute-start | bytes 393224 | tf_op jit(solution)/shard_map/ppermute | solution.py:15
  68.3 9.4 %collective-permute-start.15 = (f32[256,128]{1,0:T(8,128)S(1)}, f32[256,128]{1,0:T(8,128)S(1)}, u32[]{:S(2)}, u32[]{:S(2)}) collective-permute-start(f32[256,128]{1,0:T(8,128)S(1)} %get-tuple-element.67), channel_id=1, source_target_pairs={{0,4},{4,8},{8,12},{12,16},{16,20},{20,24},{24,28},{28,0},{1,5},{5... | collective-permute-start | bytes 393224 | tf_op jit(solution)/shard_map/ppermute | solution.py:15
  68.3 6.8 %collective-permute-start.17 = (f32[128,128]{1,0:T(8,128)S(1)}, f32[128,128]{1,0:T(8,128)S(1)}, u32[]{:S(2)}, u32[]{:S(2)}) collective-permute-start(f32[128,128]{1,0:T(8,128)S(1)} %get-tuple-element.46), channel_id=1, source_target_pairs={{0,24},{4,28},{8,0},{12,4},{16,8},{20,12},{24,16},{28,20},{1,25},{... | collective-permute-start | bytes 196616 | tf_op jit(solution)/shard_map/ppermute | solution.py:15
  70.7 7.0 %collective-permute-start.18 = (f32[128,128]{1,0:T(8,128)S(1)}, f32[128,128]{1,0:T(8,128)S(1)}, u32[]{:S(2)}, u32[]{:S(2)}) collective-permute-start(f32[128,128]{1,0:T(8,128)S(1)} %get-tuple-element.47), channel_id=1, source_target_pairs={{0,8},{4,12},{8,16},{12,20},{16,24},{20,28},{24,0},{28,4},{1,9},{5... | collective-permute-start | bytes 196616 | tf_op jit(solution)/shard_map/ppermute | solution.py:15
  78.7 4.5 %collective-permute-start.20 = (f32[128,128]{1,0:T(8,128)S(1)}, f32[128,128]{1,0:T(8,128)S(1)}, u32[]{:S(2)}, u32[]{:S(2)}) collective-permute-start(f32[128,128]{1,0:T(8,128)S(1)} %get-tuple-element.48), channel_id=1, source_target_pairs={{0,2},{1,3},{2,0},{3,1},{4,6},{5,7},{6,4},{7,5},{8,10},{9,11},{10,... | collective-permute-start | bytes 196616 | tf_op jit(solution)/shard_map/ppermute | solution.py:20
  79.7 3.9 %collective-permute-start.19 = (f32[128,128]{1,0:T(8,128)S(1)}, f32[128,128]{1,0:T(8,128)S(1)}, u32[]{:S(2)}, u32[]{:S(2)}) collective-permute-start(f32[128,128]{1,0:T(8,128)S(1)} %get-tuple-element.49), channel_id=1, source_target_pairs={{0,1},{1,2},{2,3},{3,0},{4,5},{5,6},{6,7},{7,4},{8,9},{9,10},{10,1... | collective-permute-start | bytes 196616 | tf_op jit(solution)/shard_map/ppermute | solution.py:20
  86.7 4.0 %collective-permute-start.22 = (f32[128,128]{1,0:T(8,128)}, f32[128,128]{1,0:T(8,128)S(1)}, u32[]{:S(2)}, u32[]{:S(2)}) collective-permute-start(f32[128,128]{1,0:T(8,128)} %get-tuple-element.30), channel_id=1, source_target_pairs={{0,1},{1,2},{2,3},{3,0},{4,5},{5,6},{6,7},{7,4},{8,9},{9,10},{10,1... | collective-permute-start | bytes 196616 | tf_op jit(solution)/shard_map/ppermute | solution.py:20
  86.7 5.2 %collective-permute-start.23 = (f32[128,128]{1,0:T(8,128)}, f32[128,128]{1,0:T(8,128)S(1)}, u32[]{:S(2)}, u32[]{:S(2)}) collective-permute-start(f32[128,128]{1,0:T(8,128)} %get-tuple-element.31), channel_id=1, source_target_pairs={{0,2},{1,3},{2,0},{3,1},{4,6},{5,7},{6,4},{7,5},{8,10},{9,11},{10,... | collective-permute-start | bytes 196616 | tf_op jit(solution)/shard_map/ppermute | solution.py:20
  87.8 4.1 %collective-permute-start.24 = (f32[128,128]{1,0:T(8,128)}, f32[128,128]{1,0:T(8,128)S(1)}, u32[]{:S(2)}, u32[]{:S(2)}) collective-permute-start(f32[128,128]{1,0:T(8,128)} %get-tuple-element.32), channel_id=1, source_target_pairs={{0,3},{1,0},{2,1},{3,2},{4,7},{5,4},{6,5},{7,6},{8,11},{9,8},{10,9... | collective-permute-start | bytes 196616 | tf_op jit(solution)/shard_map/ppermute | solution.py:20
  92.8 7.5 %collective-permute-start.25 = (f32[128,128]{1,0:T(8,128)S(1)}, f32[128,128]{1,0:T(8,128)S(1)}, u32[]{:S(2)}, u32[]{:S(2)}) collective-permute-start(f32[128,128]{1,0:T(8,128)S(1)} %get-tuple-element.43), channel_id=1, source_target_pairs={{0,4},{4,8},{8,12},{12,16},{16,20},{20,24},{24,28},{28,0},{1,5},{5... | collective-permute-start | bytes 196616 | tf_op jit(solution)/shard_map/ppermute | solution.py:15
  95.3 5.8 %collective-permute-start.26 = (f32[128,128]{1,0:T(8,128)S(1)}, f32[128,128]{1,0:T(8,128)S(1)}, u32[]{:S(2)}, u32[]{:S(2)}) collective-permute-start(f32[128,128]{1,0:T(8,128)S(1)} %get-tuple-element.44), channel_id=1, source_target_pairs={{0,28},{4,0},{8,4},{12,8},{16,12},{20,16},{24,20},{28,24},{1,29},{... | collective-permute-start | bytes 196616 | tf_op jit(solution)/shard_map/ppermute | solution.py:15
  (18 other events, 86.2 us)

commit v2 on v1

--- a/solution.py
+++ b/solution.py
@@ -20,9 +20,15 @@
     return lax.ppermute(block, "grp", [(i, (i + distance) % size) for i in range(size)])
 
 
-def schur_kernel(info, factor, coupling, block, high, low, fbuf, cbuf, bbuf, coupled, fsem, csem, bsem):
+def offset_of(ids, b):
+    cycles = lax.axis_size("sub")
+    owner = ids[0, b] // lax.axis_size("grp")
+    return lax.rem(owner - lax.axis_index("sub") + cycles + 1, cycles) - 1
+
+
+def schur_kernel(live, factor, coupling, block, high, low, fbuf, cbuf, bbuf, coupled, fsem, csem, bsem):
     ni, width = coupling.shape
-    nblk = info.shape[0] - 2
+    nblk = lax.axis_size("grp")
     blk = width // nblk
     steps = ni // TILE
     rows = [pl.ds(i * TILE, TILE) for i in range(steps)]
@@ -48,8 +54,8 @@
         coupled[...], coupled[...], (((0,), (0,)), ((), ())), preferred_element_type=jnp.float32
     )
     bcopy.wait()
-    member = info[0]
-    count = info[1]
+    member = lax.axis_index("grp")
+    count = live[0]
     for a in range(nblk):
         row = pl.multiple_of(lax.rem(a - member + nblk, nblk) * blk, blk)
         for b in range(nblk):
@@ -64,16 +70,16 @@
             )
 
 
-def first_kernel(info, high, low, own, near, far, *terms):
+def first_kernel(ids, high, low, own, near, far, *terms):
     nblk = len(terms)
     blk = own.shape[0] // nblk
-    member = info[0]
+    member = lax.axis_index("grp")
     even = lax.rem(member, 2) == 0
     picked = []
     for r in range(nblk):
         b = lax.rem(member - r + nblk, nblk)
         span = pl.ds(pl.multiple_of(b * blk, blk), blk)
-        dest = info[2 + b]
+        dest = offset_of(ids, b)
         use_near = jnp.logical_or(
             jnp.logical_and(dest == -1, even), jnp.logical_and(dest == 1, jnp.logical_not(even))
         )
@@ -84,7 +90,7 @@
     product = product + jnp.dot(low[...], vector, preferred_element_type=jnp.float32)
     for r in range(nblk):
         terms[r][0:blk, :] = product[r * blk : (r + 1) * blk, :]
-        dest = info[2 + lax.rem(member + r, nblk)]
+        dest = offset_of(ids, lax.rem(member + r, nblk))
         terms[r][blk : blk + TAIL, :] = jnp.full(
             (TAIL, own.shape[1]), dest.astype(jnp.float32), jnp.float32
         )
@@ -109,21 +115,18 @@
     factor = interior_factor[0]
     coupling = interface_coupling[0]
     block = interface_block[0]
-    ids = index_map[0]
-    nblk = ids.shape[0]
+    nblk = index_map.shape[1]
     ni, width = coupling.shape
     blk = width // nblk
     samples = sample_panel.shape[1]
     cycles = lax.axis_size("sub")
     groups = lax.axis_size("grp")
-    home = lax.axis_index("sub")
-    member = lax.axis_index("grp").astype(jnp.int32)
-    dest = (ids // groups - home + cycles + 1) % cycles - 1
-    info = jnp.concatenate([member[None], block_count, dest]).astype(jnp.int32)
+    assert nblk == groups
     smem = pl.BlockSpec(memory_space=pltpu.SMEM)
-    anywhere = pl.BlockSpec(memory_space=pl.ANY)
+    anywhere = pl.BlockSpec(memory_space=pltpu.HBM)
     vmem = pl.BlockSpec(memory_space=pltpu.VMEM)
 
+    small = pltpu.CompilerParams(vmem_limit_bytes=8 * 1024 * 1024)
     own = sample_panel.astype(jnp.float32)
     route = []
     for o in range(cycles):
@@ -153,10 +156,11 @@
             bytes_accessed=ni * ni + 2 * ni * width + 4 * width * width,
             transcendentals=0,
         ),
-        compiler_params=pltpu.CompilerParams(vmem_limit_bytes=32 * 1024 * 1024),
+        compiler_params=pltpu.CompilerParams(vmem_limit_bytes=52 * 1024 * 1024),
         name="schur",
-    )(info, factor, coupling, block)
-
+    )(block_count, factor, coupling, block)
+
+    near, high = lax.optimization_barrier((near, high))
     far = lax.ppermute(near, "grp", [(g, g ^ 1) for g in range(groups)])
     tall = jax.ShapeDtypeStruct((blk + TAIL, samples), jnp.float32)
     short = jax.ShapeDtypeStruct((blk, samples), jnp.float32)
@@ -165,8 +169,9 @@
         out_shape=(tall,) * nblk,
         in_specs=[smem] + [vmem] * 5,
         out_specs=(vmem,) * nblk,
+        compiler_params=small,
         name="first",
-    )(info, high, low, own, near, far)
+    )(index_map, high, low, own, near, far)
 
     owners = None
     for step in range(POWER):
@@ -176,6 +181,7 @@
                 out_shape=(short,) * nblk,
                 in_specs=[vmem] * (2 + nblk),
                 out_specs=(vmem,) * nblk,
+                compiler_params=small,
                 name="apply",
             )(high, low, *picked)
         got = [terms[0]] + [grp_shift(terms[r], r) for r in range(1, groups)]

time: 103 us -> 76.4 us (0.74)
  local copies, waits for them, and re-layouts: 9.88 us -> 0.01 us
  other arithmetic: 8.83 us -> 1.94 us
  Pallas kernels: 13.9 us -> 8.42 us
  waiting for transfers between devices: 37.2 us -> 32.6 us
    unnamed x30 -> x2, local copies, waits for them, and re-layouts: 9.88 us -> 0.01 us
    ppermute x1, waiting for transfers between devices: 5.98 us -> 0.48 us  [local(): near = lax.ppermute(own, ('sub', 'grp'), route)]
    pallas_call x2, Pallas kernels: 4.85 us -> 1.15 us  [local(): pl.pallas_call(apply_kernel, out_shape=(short,) * nblk, in_specs=[vmem] *...]
    add x4, other arithmetic: 3.54 us -> 0.17 us  [local(): sum((jnp.where(owners[r] == d, got[r], zero) for r in range(groups)))]
    ppermute x10, starting transfers between devices: 18.1 us -> 15.7 us  [sub_shift(): lax.ppermute(block, 'sub', [(i, (i + distance) % size) for i in range(siz...]
    ppermute x1, starting transfers between devices: 0.01 us -> 2.18 us  [local(): far = lax.ppermute(near, 'grp', [(g, g ^ 1) for g in range(groups)])]
    pallas_call x1, Pallas kernels: 2.52 us -> 1.01 us  [local(): pl.pallas_call(first_kernel, out_shape=(tall,) * nblk, in_specs=[smem] +...]
    select_n x4, other arithmetic: 1.37 us -> 0.11 us  [local(): chosen = jnp.where(owner == 0, here, jnp.where(owner == 1, after, before))]
  transfers between devices with their start and end apart: 27 -> 27, of which waited for: 19 -> 19; matrix products, arithmetic and copies ran while one was open for 3% -> 0% of each run, Pallas kernels for 6% -> 8%
where the time goes in v2:
time: 76.4 us; the launch traced here: 76.2 us
  waiting for transfers between devices  32.6 us (43%)
  starting transfers between devices  32.5 us (43%)
  Pallas kernels  8.42 us (11%)
  other arithmetic  1.94 us (3%)
  between operations  0.78 us (1%)
    ppermute x10, starting transfers between devices, sub_shift(): lax.ppermute(block, 'sub', [(i, (i + distance) % size) for i in range(siz...  15.7 us
    ppermute x15, waiting for transfers between devices, grp_shift(): lax.ppermute(block, 'grp', [(i, (i + distance) % size) for i in range(siz...  15.5 us
    ppermute x10, waiting for transfers between devices, sub_shift(): lax.ppermute(block, 'sub', [(i, (i + distance) % size) for i in range(siz...  15.5 us
    ppermute x15, starting transfers between devices, grp_shift(): lax.ppermute(block, 'grp', [(i, (i + distance) % size) for i in range(siz...  11.6 us
    pallas_call x1, Pallas kernels, local(): pl.pallas_call(schur_kernel, out_shape=(half, half), in_specs=[smem, anyw...  6.26 us
    ppermute x1, starting transfers between devices, local(): near = lax.ppermute(own, ('sub', 'grp'), route)  3.05 us
    ppermute x1, starting transfers between devices, local(): far = lax.ppermute(near, 'grp', [(g, g ^ 1) for g in range(groups)])  2.18 us
  transfers between devices with their start and end apart: 27, of which 19 were waited for; matrix products, arithmetic and copies ran while one was open for 0% of the time, Pallas kernels for 8%

profile of v2, /device:TPU:0, one launch (start us, length us, event | category | flops | bytes accessed | tf_op | source)
XLA Modules:
  0.0 76.2 jit_solution(8643644615384817083)
XLA Ops:
  0.9 3.0 %collective-permute-start = (f32[512,128]{1,0:T(8,128)S(1)}, f32[512,128]{1,0:T(8,128)S(1)}, u32[]{:S(2)}, u32[]{:S(2)}) collective-permute-start(f32[512,128]{1,0:T(8,128)S(1)} %convert_element_type.3.own), channel_id=1, source_target_pairs={{0,4},{1,29},{2,6},{3,31},{4,8},{5,1},{6,10},{7,3},{8,12},{9,5},{1... | collective-permute-start | bytes 786440 | tf_op jit(solution)/shard_map/ppermute | solution.py:136
  4.6 6.3 %schur.1 = (bf16[512,512]{1,0:T(8,128)(2,1)S(1)}, bf16[512,512]{1,0:T(8,128)(2,1)S(1)}) custom-call(s32[1]{0:T(128)S(6)} %copy.7.live, bf16[2048,2048]{1,0:T(8,128)(2,1)} %bitcast.27, bf16[2048,512]{1,0:T(8,128)(2,1)} %bitcast.28, f32[512,512]{1,0:T(8,128)} %bitcast.29), custom_call_target="tpu_custom_call" | custom-call | flops 3221225472 | bytes 7340032 | tf_op jit(solution)/shard_map/schur/pallas_call | solution.py:140
  11.4 2.2 %collective-permute-start.1 = (f32[512,128]{1,0:T(8,128)S(1)}, f32[512,128]{1,0:T(8,128)S(1)}, u32[]{:S(2)}, u32[]{:S(2)}) collective-permute-start(f32[512,128]{1,0:T(8,128)S(1)} %collective-permute-done.near), channel_id=1, source_target_pairs={{0,1},{1,0},{2,3},{3,2},{4,5},{5,4},{6,7},{7,6},{8,9},{9,8},{10,11... | collective-permute-start | bytes 786440 | tf_op jit(solution)/shard_map/ppermute | solution.py:164
  16.2 1.5 %collective-permute-start.3 = (f32[136,128]{1,0:T(8,128)S(1)}, f32[136,128]{1,0:T(8,128)S(1)}, u32[]{:S(2)}, u32[]{:S(2)}) collective-permute-start(f32[136,128]{1,0:T(8,128)S(1)} %get-tuple-element.27), channel_id=1, source_target_pairs={{0,2},{1,3},{2,0},{3,1},{4,6},{5,7},{6,4},{7,5},{8,10},{9,11},{10,... | collective-permute-start | bytes 208904 | tf_op jit(solution)/shard_map/ppermute | solution.py:20
  19.5 1.4 %collective-permute-done.3 = f32[136,128]{1,0:T(8,128)S(1)} collective-permute-done((f32[136,128]{1,0:T(8,128)S(1)}, f32[136,128]{1,0:T(8,128)S(1)}, u32[]{:S(2)}, u32[]{:S(2)}) %collective-permute-start.3) | collective-permute-done | bytes 69664 | tf_op jit(solution)/shard_map/ppermute | solution.py:20
  21.1 2.9 %collective-permute-start.6 = (f32[256,128]{1,0:T(8,128)S(1)}, f32[256,128]{1,0:T(8,128)S(1)}, u32[]{:S(2)}, u32[]{:S(2)}) collective-permute-start(f32[256,128]{1,0:T(8,128)S(1)} %get-tuple-element.72), channel_id=1, source_target_pairs={{0,28},{4,0},{8,4},{12,8},{16,12},{20,16},{24,20},{28,24},{1,29},{... | collective-permute-start | bytes 393224 | tf_op jit(solution)/shard_map/ppermute | solution.py:15
  24.0 3.8 %collective-permute-start.7 = (f32[128,128]{1,0:T(8,128)S(1)}, f32[128,128]{1,0:T(8,128)S(1)}, u32[]{:S(2)}, u32[]{:S(2)}) collective-permute-start(f32[128,128]{1,0:T(8,128)S(1)} %select_add_fusion.5), channel_id=1, source_target_pairs={{0,24},{4,28},{8,0},{12,4},{16,8},{20,12},{24,16},{28,20},{1,25},{... | collective-permute-start | bytes 196616 | tf_op jit(solution)/shard_map/ppermute | solution.py:15
  27.8 2.9 %collective-permute-done.8 = f32[128,128]{1,0:T(8,128)S(1)} collective-permute-done((f32[128,128]{1,0:T(8,128)S(1)}, f32[128,128]{1,0:T(8,128)S(1)}, u32[]{:S(2)}, u32[]{:S(2)}) %collective-permute-start.8) | collective-permute-done | bytes 65568 | tf_op jit(solution)/shard_map/ppermute | solution.py:15
  30.7 2.4 %collective-permute-done.5 = f32[256,128]{1,0:T(8,128)S(1)} collective-permute-done((f32[256,128]{1,0:T(8,128)S(1)}, f32[256,128]{1,0:T(8,128)S(1)}, u32[]{:S(2)}, u32[]{:S(2)}) %collective-permute-start.5) | collective-permute-done | bytes 131104 | tf_op jit(solution)/shard_map/ppermute | solution.py:15
  33.3 1.8 %collective-permute-start.10 = (f32[128,128]{1,0:T(8,128)S(1)}, f32[128,128]{1,0:T(8,128)S(1)}, u32[]{:S(2)}, u32[]{:S(2)}) collective-permute-start(f32[128,128]{1,0:T(8,128)S(1)} %get-tuple-element.55), channel_id=1, source_target_pairs={{0,2},{1,3},{2,0},{3,1},{4,6},{5,7},{6,4},{7,5},{8,10},{9,11},{10,... | collective-permute-start | bytes 196616 | tf_op jit(solution)/shard_map/ppermute | solution.py:20
  35.3 3.7 %collective-permute-done.10.refs_2_ = f32[128,128]{1,0:T(8,128)S(1)} collective-permute-done((f32[128,128]{1,0:T(8,128)S(1)}, f32[128,128]{1,0:T(8,128)S(1)}, u32[]{:S(2)}, u32[]{:S(2)}) %collective-permute-start.10) | collective-permute-done | bytes 65568 | tf_op jit(solution)/shard_map/ppermute | solution.py:20
  41.0 1.4 %collective-permute-start.14 = (f32[128,128]{1,0:T(8,128)S(1)}, f32[128,128]{1,0:T(8,128)S(1)}, u32[]{:S(2)}, u32[]{:S(2)}) collective-permute-start(f32[128,128]{1,0:T(8,128)S(1)} %get-tuple-element.32), channel_id=1, source_target_pairs={{0,3},{1,0},{2,1},{3,2},{4,7},{5,4},{6,5},{7,6},{8,11},{9,8},{10,9... | collective-permute-start | bytes 196616 | tf_op jit(solution)/shard_map/ppermute | solution.py:20
  42.3 1.2 %collective-permute-done.12 = f32[128,128]{1,0:T(8,128)S(1)} collective-permute-done((f32[128,128]{1,0:T(8,128)S(1)}, f32[128,128]{1,0:T(8,128)S(1)}, u32[]{:S(2)}, u32[]{:S(2)}) %collective-permute-start.12) | collective-permute-done | bytes 65568 | tf_op jit(solution)/shard_map/ppermute | solution.py:20
  43.6 1.3 %collective-permute-done.13 = f32[128,128]{1,0:T(8,128)S(1)} collective-permute-done((f32[128,128]{1,0:T(8,128)S(1)}, f32[128,128]{1,0:T(8,128)S(1)}, u32[]{:S(2)}, u32[]{:S(2)}) %collective-permute-start.13) | collective-permute-done | bytes 65568 | tf_op jit(solution)/shard_map/ppermute | solution.py:20
  45.0 1.7 %collective-permute-start.16 = (f32[256,128]{1,0:T(8,128)S(1)}, f32[256,128]{1,0:T(8,128)S(1)}, u32[]{:S(2)}, u32[]{:S(2)}) collective-permute-start(f32[256,128]{1,0:T(8,128)S(1)} %get-tuple-element.70), channel_id=1, source_target_pairs={{0,28},{4,0},{8,4},{12,8},{16,12},{20,16},{24,20},{28,24},{1,29},{... | collective-permute-start | bytes 393224 | tf_op jit(solution)/shard_map/ppermute | solution.py:15
  47.1 2.1 %collective-permute-start.17 = (f32[128,128]{1,0:T(8,128)S(1)}, f32[128,128]{1,0:T(8,128)S(1)}, u32[]{:S(2)}, u32[]{:S(2)}) collective-permute-start(f32[128,128]{1,0:T(8,128)S(1)} %get-tuple-element.50), channel_id=1, source_target_pairs={{0,24},{4,28},{8,0},{12,4},{16,8},{20,12},{24,16},{28,20},{1,25},{... | collective-permute-start | bytes 196616 | tf_op jit(solution)/shard_map/ppermute | solution.py:15
  49.2 4.6 %collective-permute-done.17 = f32[128,128]{1,0:T(8,128)S(1)} collective-permute-done((f32[128,128]{1,0:T(8,128)S(1)}, f32[128,128]{1,0:T(8,128)S(1)}, u32[]{:S(2)}, u32[]{:S(2)}) %collective-permute-start.17) | collective-permute-done | bytes 65568 | tf_op jit(solution)/shard_map/ppermute | solution.py:15
  53.8 2.3 %collective-permute-done.18 = f32[128,128]{1,0:T(8,128)S(1)} collective-permute-done((f32[128,128]{1,0:T(8,128)S(1)}, f32[128,128]{1,0:T(8,128)S(1)}, u32[]{:S(2)}, u32[]{:S(2)}) %collective-permute-start.18) | collective-permute-done | bytes 65568 | tf_op jit(solution)/shard_map/ppermute | solution.py:15
  58.6 3.0 %collective-permute-done.20.refs_2_ = f32[128,128]{1,0:T(8,128)S(1)} collective-permute-done((f32[128,128]{1,0:T(8,128)S(1)}, f32[128,128]{1,0:T(8,128)S(1)}, u32[]{:S(2)}, u32[]{:S(2)}) %collective-permute-start.20) | collective-permute-done | bytes 65568 | tf_op jit(solution)/shard_map/ppermute | solution.py:20
  63.6 1.4 %collective-permute-start.24 = (f32[128,128]{1,0:T(8,128)S(1)}, f32[128,128]{1,0:T(8,128)S(1)}, u32[]{:S(2)}, u32[]{:S(2)}) collective-permute-start(f32[128,128]{1,0:T(8,128)S(1)} %get-tuple-element.36), channel_id=1, source_target_pairs={{0,3},{1,0},{2,1},{3,2},{4,7},{5,4},{6,5},{7,6},{8,11},{9,8},{10,9... | collective-permute-start | bytes 196616 | tf_op jit(solution)/shard_map/ppermute | solution.py:20
  66.2 1.3 %collective-permute-done.23 = f32[128,128]{1,0:T(8,128)S(1)} collective-permute-done((f32[128,128]{1,0:T(8,128)S(1)}, f32[128,128]{1,0:T(8,128)S(1)}, u32[]{:S(2)}, u32[]{:S(2)}) %collective-permute-start.23) | collective-permute-done | bytes 65568 | tf_op jit(solution)/shard_map/ppermute | solution.py:20
  67.6 2.3 %collective-permute-start.25 = (f32[128,128]{1,0:T(8,128)S(1)}, f32[128,128]{1,0:T(8,128)S(1)}, u32[]{:S(2)}, u32[]{:S(2)}) collective-permute-start(f32[128,128]{1,0:T(8,128)S(1)} %get-tuple-element.47), channel_id=1, source_target_pairs={{0,4},{4,8},{8,12},{12,16},{16,20},{20,24},{24,28},{28,0},{1,5},{5... | collective-permute-start | bytes 196616 | tf_op jit(solution)/shard_map/ppermute | solution.py:15
  69.9 2.5 %collective-permute-start.26 = (f32[128,128]{1,0:T(8,128)S(1)}, f32[128,128]{1,0:T(8,128)S(1)}, u32[]{:S(2)}, u32[]{:S(2)}) collective-permute-start(f32[128,128]{1,0:T(8,128)S(1)} %get-tuple-element.48), channel_id=1, source_target_pairs={{0,28},{4,0},{8,4},{12,8},{16,12},{20,16},{24,20},{28,24},{1,29},{... | collective-permute-start | bytes 196616 | tf_op jit(solution)/shard_map/ppermute | solution.py:15
  72.4 2.6 %collective-permute-done.25 = f32[128,128]{1,0:T(8,128)S(1)} collective-permute-done((f32[128,128]{1,0:T(8,128)S(1)}, f32[128,128]{1,0:T(8,128)S(1)}, u32[]{:S(2)}, u32[]{:S(2)}) %collective-permute-start.25) | collective-permute-done | bytes 65568 | tf_op jit(solution)/shard_map/ppermute | solution.py:15
  (52 shorter events, 15.7 us)
Async XLA Ops:
  0.9 10.4 %collective-permute-start = (f32[512,128]{1,0:T(8,128)S(1)}, f32[512,128]{1,0:T(8,128)S(1)}, u32[]{:S(2)}, u32[]{:S(2)}) collective-permute-start(f32[512,128]{1,0:T(8,128)S(1)} %convert_element_type.3.own), channel_id=1, source_target_pairs={{0,4},{1,29},{2,6},{3,31},{4,8},{5,1},{6,10},{7,3},{8,12},{9,5},{1... | collective-permute-start | bytes 786440 | tf_op jit(solution)/shard_map/ppermute | solution.py:136
  11.4 3.3 %collective-permute-start.1 = (f32[512,128]{1,0:T(8,128)S(1)}, f32[512,128]{1,0:T(8,128)S(1)}, u32[]{:S(2)}, u32[]{:S(2)}) collective-permute-start(f32[512,128]{1,0:T(8,128)S(1)} %collective-permute-done.near), channel_id=1, source_target_pairs={{0,1},{1,0},{2,3},{3,2},{4,5},{5,4},{6,7},{7,6},{8,9},{9,8},{10,11... | collective-permute-start | bytes 786440 | tf_op jit(solution)/shard_map/ppermute | solution.py:164
  15.7 3.8 %collective-permute-start.2 = (f32[136,128]{1,0:T(8,128)S(1)}, f32[136,128]{1,0:T(8,128)S(1)}, u32[]{:S(2)}, u32[]{:S(2)}) collective-permute-start(f32[136,128]{1,0:T(8,128)S(1)} %get-tuple-element.26), channel_id=1, source_target_pairs={{0,1},{1,2},{2,3},{3,0},{4,5},{5,6},{6,7},{7,4},{8,9},{9,10},{10,1... | collective-permute-start | bytes 208904 | tf_op jit(solution)/shard_map/ppermute | solution.py:20
  16.2 4.8 %collective-permute-start.3 = (f32[136,128]{1,0:T(8,128)S(1)}, f32[136,128]{1,0:T(8,128)S(1)}, u32[]{:S(2)}, u32[]{:S(2)}) collective-permute-start(f32[136,128]{1,0:T(8,128)S(1)} %get-tuple-element.27), channel_id=1, source_target_pairs={{0,2},{1,3},{2,0},{3,1},{4,6},{5,7},{6,4},{7,5},{8,10},{9,11},{10,... | collective-permute-start | bytes 208904 | tf_op jit(solution)/shard_map/ppermute | solution.py:20
  21.1 9.6 %collective-permute-start.6 = (f32[256,128]{1,0:T(8,128)S(1)}, f32[256,128]{1,0:T(8,128)S(1)}, u32[]{:S(2)}, u32[]{:S(2)}) collective-permute-start(f32[256,128]{1,0:T(8,128)S(1)} %get-tuple-element.72), channel_id=1, source_target_pairs={{0,28},{4,0},{8,4},{12,8},{16,12},{20,16},{24,20},{28,24},{1,29},{... | collective-permute-start | bytes 393224 | tf_op jit(solution)/shard_map/ppermute | solution.py:15
  24.0 9.2 %collective-permute-start.5 = (f32[256,128]{1,0:T(8,128)S(1)}, f32[256,128]{1,0:T(8,128)S(1)}, u32[]{:S(2)}, u32[]{:S(2)}) collective-permute-start(f32[256,128]{1,0:T(8,128)S(1)} %get-tuple-element.73), channel_id=1, source_target_pairs={{0,4},{4,8},{8,12},{12,16},{16,20},{20,24},{24,28},{28,0},{1,5},{5... | collective-permute-start | bytes 393224 | tf_op jit(solution)/shard_map/ppermute | solution.py:15
  24.0 6.8 %collective-permute-start.8 = (f32[128,128]{1,0:T(8,128)S(1)}, f32[128,128]{1,0:T(8,128)S(1)}, u32[]{:S(2)}, u32[]{:S(2)}) collective-permute-start(f32[128,128]{1,0:T(8,128)S(1)} %get-tuple-element.46), channel_id=1, source_target_pairs={{0,8},{4,12},{8,16},{12,20},{16,24},{20,28},{24,0},{28,4},{1,9},{5... | collective-permute-start | bytes 196616 | tf_op jit(solution)/shard_map/ppermute | solution.py:15
  24.0 6.8 %collective-permute-start.7 = (f32[128,128]{1,0:T(8,128)S(1)}, f32[128,128]{1,0:T(8,128)S(1)}, u32[]{:S(2)}, u32[]{:S(2)}) collective-permute-start(f32[128,128]{1,0:T(8,128)S(1)} %select_add_fusion.5), channel_id=1, source_target_pairs={{0,24},{4,28},{8,0},{12,4},{16,8},{20,12},{24,16},{28,20},{1,25},{... | collective-permute-start | bytes 196616 | tf_op jit(solution)/shard_map/ppermute | solution.py:15
  33.3 5.7 %collective-permute-start.10 = (f32[128,128]{1,0:T(8,128)S(1)}, f32[128,128]{1,0:T(8,128)S(1)}, u32[]{:S(2)}, u32[]{:S(2)}) collective-permute-start(f32[128,128]{1,0:T(8,128)S(1)} %get-tuple-element.55), channel_id=1, source_target_pairs={{0,2},{1,3},{2,0},{3,1},{4,6},{5,7},{6,4},{7,5},{8,10},{9,11},{10,... | collective-permute-start | bytes 196616 | tf_op jit(solution)/shard_map/ppermute | solution.py:20
  35.1 4.2 %collective-permute-start.9 = (f32[128,128]{1,0:T(8,128)S(1)}, f32[128,128]{1,0:T(8,128)S(1)}, u32[]{:S(2)}, u32[]{:S(2)}) collective-permute-start(f32[128,128]{1,0:T(8,128)S(1)} %get-tuple-element.56), channel_id=1, source_target_pairs={{0,1},{1,2},{2,3},{3,0},{4,5},{5,6},{6,7},{7,4},{8,9},{9,10},{10,1... | collective-permute-start | bytes 196616 | tf_op jit(solution)/shard_map/ppermute | solution.py:20
  39.8 3.8 %collective-permute-start.12 = (f32[128,128]{1,0:T(8,128)S(1)}, f32[128,128]{1,0:T(8,128)S(1)}, u32[]{:S(2)}, u32[]{:S(2)}) collective-permute-start(f32[128,128]{1,0:T(8,128)S(1)} %get-tuple-element.30), channel_id=1, source_target_pairs={{0,1},{1,2},{2,3},{3,0},{4,5},{5,6},{6,7},{7,4},{8,9},{9,10},{10,1... | collective-permute-start | bytes 196616 | tf_op jit(solution)/shard_map/ppermute | solution.py:20
  39.9 5.0 %collective-permute-start.13 = (f32[128,128]{1,0:T(8,128)S(1)}, f32[128,128]{1,0:T(8,128)S(1)}, u32[]{:S(2)}, u32[]{:S(2)}) collective-permute-start(f32[128,128]{1,0:T(8,128)S(1)} %get-tuple-element.31), channel_id=1, source_target_pairs={{0,2},{1,3},{2,0},{3,1},{4,6},{5,7},{6,4},{7,5},{8,10},{9,11},{10,... | collective-permute-start | bytes 196616 | tf_op jit(solution)/shard_map/ppermute | solution.py:20
  41.0 3.9 %collective-permute-start.14 = (f32[128,128]{1,0:T(8,128)S(1)}, f32[128,128]{1,0:T(8,128)S(1)}, u32[]{:S(2)}, u32[]{:S(2)}) collective-permute-start(f32[128,128]{1,0:T(8,128)S(1)} %get-tuple-element.32), channel_id=1, source_target_pairs={{0,3},{1,0},{2,1},{3,2},{4,7},{5,4},{6,5},{7,6},{8,11},{9,8},{10,9... | collective-permute-start | bytes 196616 | tf_op jit(solution)/shard_map/ppermute | solution.py:20
  45.0 11.1 %collective-permute-start.16 = (f32[256,128]{1,0:T(8,128)S(1)}, f32[256,128]{1,0:T(8,128)S(1)}, u32[]{:S(2)}, u32[]{:S(2)}) collective-permute-start(f32[256,128]{1,0:T(8,128)S(1)} %get-tuple-element.70), channel_id=1, source_target_pairs={{0,28},{4,0},{8,4},{12,8},{16,12},{20,16},{24,20},{28,24},{1,29},{... | collective-permute-start | bytes 393224 | tf_op jit(solution)/shard_map/ppermute | solution.py:15
  46.7 9.4 %collective-permute-start.15 = (f32[256,128]{1,0:T(8,128)S(1)}, f32[256,128]{1,0:T(8,128)S(1)}, u32[]{:S(2)}, u32[]{:S(2)}) collective-permute-start(f32[256,128]{1,0:T(8,128)S(1)} %get-tuple-element.71), channel_id=1, source_target_pairs={{0,4},{4,8},{8,12},{12,16},{16,20},{20,24},{24,28},{28,0},{1,5},{5... | collective-permute-start | bytes 393224 | tf_op jit(solution)/shard_map/ppermute | solution.py:15
  47.1 6.8 %collective-permute-start.17 = (f32[128,128]{1,0:T(8,128)S(1)}, f32[128,128]{1,0:T(8,128)S(1)}, u32[]{:S(2)}, u32[]{:S(2)}) collective-permute-start(f32[128,128]{1,0:T(8,128)S(1)} %get-tuple-element.50), channel_id=1, source_target_pairs={{0,24},{4,28},{8,0},{12,4},{16,8},{20,12},{24,16},{28,20},{1,25},{... | collective-permute-start | bytes 196616 | tf_op jit(solution)/shard_map/ppermute | solution.py:15
  49.2 6.9 %collective-permute-start.18 = (f32[128,128]{1,0:T(8,128)S(1)}, f32[128,128]{1,0:T(8,128)S(1)}, u32[]{:S(2)}, u32[]{:S(2)}) collective-permute-start(f32[128,128]{1,0:T(8,128)S(1)} %get-tuple-element.51), channel_id=1, source_target_pairs={{0,8},{4,12},{8,16},{12,20},{16,24},{20,28},{24,0},{28,4},{1,9},{5... | collective-permute-start | bytes 196616 | tf_op jit(solution)/shard_map/ppermute | solution.py:15
  56.5 5.0 %collective-permute-start.20 = (f32[128,128]{1,0:T(8,128)S(1)}, f32[128,128]{1,0:T(8,128)S(1)}, u32[]{:S(2)}, u32[]{:S(2)}) collective-permute-start(f32[128,128]{1,0:T(8,128)S(1)} %get-tuple-element.52), channel_id=1, source_target_pairs={{0,2},{1,3},{2,0},{3,1},{4,6},{5,7},{6,4},{7,5},{8,10},{9,11},{10,... | collective-permute-start | bytes 196616 | tf_op jit(solution)/shard_map/ppermute | solution.py:20
  57.6 4.3 %collective-permute-start.19 = (f32[128,128]{1,0:T(8,128)S(1)}, f32[128,128]{1,0:T(8,128)S(1)}, u32[]{:S(2)}, u32[]{:S(2)}) collective-permute-start(f32[128,128]{1,0:T(8,128)S(1)} %get-tuple-element.53), channel_id=1, source_target_pairs={{0,1},{1,2},{2,3},{3,0},{4,5},{5,6},{6,7},{7,4},{8,9},{9,10},{10,1... | collective-permute-start | bytes 196616 | tf_op jit(solution)/shard_map/ppermute | solution.py:20
  62.4 3.8 %collective-permute-start.22 = (f32[128,128]{1,0:T(8,128)S(1)}, f32[128,128]{1,0:T(8,128)S(1)}, u32[]{:S(2)}, u32[]{:S(2)}) collective-permute-start(f32[128,128]{1,0:T(8,128)S(1)} %get-tuple-element.34), channel_id=1, source_target_pairs={{0,1},{1,2},{2,3},{3,0},{4,5},{5,6},{6,7},{7,4},{8,9},{9,10},{10,1... | collective-permute-start | bytes 196616 | tf_op jit(solution)/shard_map/ppermute | solution.py:20
  62.5 5.0 %collective-permute-start.23 = (f32[128,128]{1,0:T(8,128)S(1)}, f32[128,128]{1,0:T(8,128)S(1)}, u32[]{:S(2)}, u32[]{:S(2)}) collective-permute-start(f32[128,128]{1,0:T(8,128)S(1)} %get-tuple-element.35), channel_id=1, source_target_pairs={{0,2},{1,3},{2,0},{3,1},{4,6},{5,7},{6,4},{7,5},{8,10},{9,11},{10,... | collective-permute-start | bytes 196616 | tf_op jit(solution)/shard_map/ppermute | solution.py:20
  63.6 3.9 %collective-permute-start.24 = (f32[128,128]{1,0:T(8,128)S(1)}, f32[128,128]{1,0:T(8,128)S(1)}, u32[]{:S(2)}, u32[]{:S(2)}) collective-permute-start(f32[128,128]{1,0:T(8,128)S(1)} %get-tuple-element.36), channel_id=1, source_target_pairs={{0,3},{1,0},{2,1},{3,2},{4,7},{5,4},{6,5},{7,6},{8,11},{9,8},{10,9... | collective-permute-start | bytes 196616 | tf_op jit(solution)/shard_map/ppermute | solution.py:20
  67.6 7.4 %collective-permute-start.25 = (f32[128,128]{1,0:T(8,128)S(1)}, f32[128,128]{1,0:T(8,128)S(1)}, u32[]{:S(2)}, u32[]{:S(2)}) collective-permute-start(f32[128,128]{1,0:T(8,128)S(1)} %get-tuple-element.47), channel_id=1, source_target_pairs={{0,4},{4,8},{8,12},{12,16},{16,20},{20,24},{24,28},{28,0},{1,5},{5... | collective-permute-start | bytes 196616 | tf_op jit(solution)/shard_map/ppermute | solution.py:15
  69.9 5.7 %collective-permute-start.26 = (f32[128,128]{1,0:T(8,128)S(1)}, f32[128,128]{1,0:T(8,128)S(1)}, u32[]{:S(2)}, u32[]{:S(2)}) collective-permute-start(f32[128,128]{1,0:T(8,128)S(1)} %get-tuple-element.48), channel_id=1, source_target_pairs={{0,28},{4,0},{8,4},{12,8},{16,12},{20,16},{24,20},{28,24},{1,29},{... | collective-permute-start | bytes 196616 | tf_op jit(solution)/shard_map/ppermute | solution.py:15
  (4 other events, 22.5 us)

commit v3 on v2

--- a/solution.py
+++ b/solution.py
@@ -24,6 +24,21 @@
     cycles = lax.axis_size("sub")
     owner = ids[0, b] // lax.axis_size("grp")
     return lax.rem(owner - lax.axis_index("sub") + cycles + 1, cycles) - 1
+
+
+def cross_shift(forward, backward, distance, even):
+    size = lax.axis_size("sub")
+    groups = lax.axis_size("grp")
+    got = []
+    for sign in (1, -1):
+        route = []
+        for o in range(size):
+            for g in range(groups):
+                step = sign * distance * (1 if g % 2 == 0 else -1)
+                route.append((o * groups + g, ((o + step) % size) * groups + g))
+        first, second = (forward, backward) if sign == 1 else (backward, forward)
+        got.append(lax.ppermute(jnp.where(even, first, second), ("sub", "grp"), route))
+    return jnp.where(even, got[0], got[1]), jnp.where(even, got[1], got[0])
 
 
 def schur_kernel(live, factor, coupling, block, high, low, fbuf, cbuf, bbuf, coupled, fsem, csem, bsem):
@@ -174,6 +189,7 @@
     )(index_map, high, low, own, near, far)
 
     owners = None
+    even = lax.axis_index("grp") % 2 == 0
     for step in range(POWER):
         if step > 0:
             terms = pl.pallas_call(
@@ -193,8 +209,9 @@
         for d in (-1, 0, 1):
             sums[d] = sum(jnp.where(owners[r] == d, got[r], zero) for r in range(groups))
         if step + 1 < POWER:
-            behind = sub_shift(jnp.concatenate([sums[0], sums[1]]), 1)
-            ahead = sub_shift(jnp.concatenate([sums[0], sums[-1]]), -1)
+            behind, ahead = cross_shift(
+                jnp.concatenate([sums[0], sums[1]]), jnp.concatenate([sums[0], sums[-1]]), 1, even
+            )
             behind2 = sub_shift(sums[1], 2)
             ahead2 = sub_shift(sums[-1], -2)
             here = sums[0] + behind[blk:] + ahead[blk:]

time: 76.4 us -> 74 us (0.969)
  waiting for transfers between devices: 32.6 us -> 26.1 us
  starting transfers between devices: 32.5 us -> 36.6 us
    ppermute x0 -> x4, starting transfers between devices: none -> 9.54 us  [cross_shift(): lax.ppermute(jnp.where(even, first, second), ('sub', 'grp'), route)]
    ppermute x10 -> x6, waiting for transfers between devices: 15.5 us -> 8.04 us  [sub_shift(): lax.ppermute(block, 'sub', [(i, (i + distance) % size) for i in range(siz...]
    ppermute x10 -> x6, starting transfers between devices: 15.7 us -> 8.83 us  [sub_shift(): lax.ppermute(block, 'sub', [(i, (i + distance) % size) for i in range(siz...]
    ppermute x0 -> x4, waiting for transfers between devices: none -> 2.48 us  [cross_shift(): lax.ppermute(jnp.where(even, first, second), ('sub', 'grp'), route)]
    ppermute x15, waiting for transfers between devices: 15.5 us -> 14 us  [grp_shift(): lax.ppermute(block, 'grp', [(i, (i + distance) % size) for i in range(siz...]
    ppermute x15, starting transfers between devices: 11.6 us -> 13 us  [grp_shift(): lax.ppermute(block, 'grp', [(i, (i + distance) % size) for i in range(siz...]
  transfers between devices with their start and end apart: 27 -> 27, of which waited for: 19 -> 20; matrix products, arithmetic and copies ran while one was open for 0% -> 0% of each run, Pallas kernels for 8% -> 8%
where the time goes in v3:
time: 74 us; the launch traced here: 73.9 us
  starting transfers between devices  36.6 us (49%)
  waiting for transfers between devices  26.1 us (35%)
  Pallas kernels  8.42 us (11%)
  other arithmetic  1.98 us (3%)
  between operations  0.78 us (1%)
    ppermute x15, waiting for transfers between devices, grp_shift(): lax.ppermute(block, 'grp', [(i, (i + distance) % size) for i in range(siz...  14 us
    ppermute x15, starting transfers between devices, grp_shift(): lax.ppermute(block, 'grp', [(i, (i + distance) % size) for i in range(siz...  13 us
    ppermute x4, starting transfers between devices, cross_shift(): lax.ppermute(jnp.where(even, first, second), ('sub', 'grp'), route)  9.54 us
    ppermute x6, starting transfers between devices, sub_shift(): lax.ppermute(block, 'sub', [(i, (i + distance) % size) for i in range(siz...  8.83 us
    ppermute x6, waiting for transfers between devices, sub_shift(): lax.ppermute(block, 'sub', [(i, (i + distance) % size) for i in range(siz...  8.04 us
    pallas_call x1, Pallas kernels, local(): pl.pallas_call(schur_kernel, out_shape=(half, half), in_specs=[smem, anyw...  6.26 us
    ppermute x1, starting transfers between devices, local(): near = lax.ppermute(own, ('sub', 'grp'), route)  3.05 us
    ppermute x4, waiting for transfers between devices, cross_shift(): lax.ppermute(jnp.where(even, first, second), ('sub', 'grp'), route)  2.48 us
  transfers between devices with their start and end apart: 27, of which 20 were waited for; matrix products, arithmetic and copies ran while one was open for 0% of the time, Pallas kernels for 8%

profile of v3, /device:TPU:0, one launch (start us, length us, event | category | flops | bytes accessed | tf_op | source)
XLA Modules:
  0.0 73.9 jit_solution(15063867917340345507)
XLA Ops:
  0.9 3.0 %collective-permute-start = (f32[512,128]{1,0:T(8,128)S(1)}, f32[512,128]{1,0:T(8,128)S(1)}, u32[]{:S(2)}, u32[]{:S(2)}) collective-permute-start(f32[512,128]{1,0:T(8,128)S(1)} %convert_element_type.3.own), channel_id=1, source_target_pairs={{0,4},{1,29},{2,6},{3,31},{4,8},{5,1},{6,10},{7,3},{8,12},{9,5},{1... | collective-permute-start | bytes 786440 | tf_op jit(solution)/shard_map/ppermute | solution.py:151
  4.6 6.3 %schur.1 = (bf16[512,512]{1,0:T(8,128)(2,1)S(1)}, bf16[512,512]{1,0:T(8,128)(2,1)S(1)}) custom-call(s32[1]{0:T(128)S(6)} %copy.7.live, bf16[2048,2048]{1,0:T(8,128)(2,1)} %bitcast.27, bf16[2048,512]{1,0:T(8,128)(2,1)} %bitcast.28, f32[512,512]{1,0:T(8,128)} %bitcast.29), custom_call_target="tpu_custom_call" | custom-call | flops 3221225472 | bytes 7340032 | tf_op jit(solution)/shard_map/schur/pallas_call | solution.py:155
  11.4 2.2 %collective-permute-start.1 = (f32[512,128]{1,0:T(8,128)S(1)}, f32[512,128]{1,0:T(8,128)S(1)}, u32[]{:S(2)}, u32[]{:S(2)}) collective-permute-start(f32[512,128]{1,0:T(8,128)S(1)} %collective-permute-done.near), channel_id=1, source_target_pairs={{0,1},{1,0},{2,3},{3,2},{4,5},{5,4},{6,7},{7,6},{8,9},{9,8},{10,11... | collective-permute-start | bytes 786440 | tf_op jit(solution)/shard_map/ppermute | solution.py:179
  15.7 1.6 %collective-permute-start.3 = (f32[136,128]{1,0:T(8,128)S(1)}, f32[136,128]{1,0:T(8,128)S(1)}, u32[]{:S(2)}, u32[]{:S(2)}) collective-permute-start(f32[136,128]{1,0:T(8,128)S(1)} %get-tuple-element.27), channel_id=1, source_target_pairs={{0,2},{1,3},{2,0},{3,1},{4,6},{5,7},{6,4},{7,5},{8,10},{9,11},{10,... | collective-permute-start | bytes 208904 | tf_op jit(solution)/shard_map/ppermute | solution.py:20
  17.8 2.5 %collective-permute-done.3 = f32[136,128]{1,0:T(8,128)S(1)} collective-permute-done((f32[136,128]{1,0:T(8,128)S(1)}, f32[136,128]{1,0:T(8,128)S(1)}, u32[]{:S(2)}, u32[]{:S(2)}) %collective-permute-start.3) | collective-permute-done | bytes 69664 | tf_op jit(solution)/shard_map/ppermute | solution.py:20
  20.5 1.5 %collective-permute-done.2 = f32[136,128]{1,0:T(8,128)S(1)} collective-permute-done((f32[136,128]{1,0:T(8,128)S(1)}, f32[136,128]{1,0:T(8,128)S(1)}, u32[]{:S(2)}, u32[]{:S(2)}) %collective-permute-start.2) | collective-permute-done | bytes 69664 | tf_op jit(solution)/shard_map/ppermute | solution.py:20
  22.2 4.7 %collective-permute-start.6 = (f32[256,128]{1,0:T(8,128)S(1)}, f32[256,128]{1,0:T(8,128)S(1)}, u32[]{:S(2)}, u32[]{:S(2)}) collective-permute-start(f32[256,128]{1,0:T(8,128)S(1)} %get-tuple-element.64), channel_id=1, source_target_pairs={{0,28},{1,5},{2,30},{3,7},{4,0},{5,9},{6,2},{7,11},{8,4},{9,13},{1... | collective-permute-start | bytes 393224 | tf_op jit(solution)/shard_map/ppermute | solution.py:40
  26.9 2.0 %collective-permute-start.8 = (f32[128,128]{1,0:T(8,128)S(1)}, f32[128,128]{1,0:T(8,128)S(1)}, u32[]{:S(2)}, u32[]{:S(2)}) collective-permute-start(f32[128,128]{1,0:T(8,128)S(1)} %get-tuple-element.46), channel_id=1, source_target_pairs={{0,8},{4,12},{8,16},{12,20},{16,24},{20,28},{24,0},{28,4},{1,9},{5... | collective-permute-start | bytes 196616 | tf_op jit(solution)/shard_map/ppermute | solution.py:15
  29.9 1.4 %collective-permute-done.7 = f32[128,128]{1,0:T(8,128)S(1)} collective-permute-done((f32[128,128]{1,0:T(8,128)S(1)}, f32[128,128]{1,0:T(8,128)S(1)}, u32[]{:S(2)}, u32[]{:S(2)}) %collective-permute-start.7) | collective-permute-done | bytes 65568 | tf_op jit(solution)/shard_map/ppermute | solution.py:15
  31.4 1.5 %collective-permute-done.8 = f32[128,128]{1,0:T(8,128)S(1)} collective-permute-done((f32[128,128]{1,0:T(8,128)S(1)}, f32[128,128]{1,0:T(8,128)S(1)}, u32[]{:S(2)}, u32[]{:S(2)}) %collective-permute-start.8) | collective-permute-done | bytes 65568 | tf_op jit(solution)/shard_map/ppermute | solution.py:15
  33.0 1.3 %collective-permute-start.10 = (f32[128,128]{1,0:T(8,128)S(1)}, f32[128,128]{1,0:T(8,128)S(1)}, u32[]{:S(2)}, u32[]{:S(2)}) collective-permute-start(f32[128,128]{1,0:T(8,128)S(1)} %get-tuple-element.61), channel_id=1, source_target_pairs={{0,2},{1,3},{2,0},{3,1},{4,6},{5,7},{6,4},{7,5},{8,10},{9,11},{10,... | collective-permute-start | bytes 196616 | tf_op jit(solution)/shard_map/ppermute | solution.py:20
  34.3 1.7 %collective-permute-start.11 = (f32[128,128]{1,0:T(8,128)S(1)}, f32[128,128]{1,0:T(8,128)S(1)}, u32[]{:S(2)}, u32[]{:S(2)}) collective-permute-start(f32[128,128]{1,0:T(8,128)S(1)} %get-tuple-element.41), channel_id=1, source_target_pairs={{0,3},{1,0},{2,1},{3,2},{4,7},{5,4},{6,5},{7,6},{8,11},{9,8},{10,9... | collective-permute-start | bytes 196616 | tf_op jit(solution)/shard_map/ppermute | solution.py:20
  42.4 1.7 %collective-permute-done.13 = f32[128,128]{1,0:T(8,128)S(1)} collective-permute-done((f32[128,128]{1,0:T(8,128)S(1)}, f32[128,128]{1,0:T(8,128)S(1)}, u32[]{:S(2)}, u32[]{:S(2)}) %collective-permute-start.13) | collective-permute-done | bytes 65568 | tf_op jit(solution)/shard_map/ppermute | solution.py:20
  44.1 1.3 %collective-permute-start.15 = (f32[256,128]{1,0:T(8,128)S(1)}, f32[256,128]{1,0:T(8,128)S(1)}, u32[]{:S(2)}, u32[]{:S(2)}) collective-permute-start(f32[256,128]{1,0:T(8,128)S(1)} %get-tuple-element.60), channel_id=1, source_target_pairs={{0,4},{1,29},{2,6},{3,31},{4,8},{5,1},{6,10},{7,3},{8,12},{9,5},{1... | collective-permute-start | bytes 393224 | tf_op jit(solution)/shard_map/ppermute | solution.py:40
  45.4 3.5 %collective-permute-start.16 = (f32[256,128]{1,0:T(8,128)S(1)}, f32[256,128]{1,0:T(8,128)S(1)}, u32[]{:S(2)}, u32[]{:S(2)}) collective-permute-start(f32[256,128]{1,0:T(8,128)S(1)} %get-tuple-element.59), channel_id=1, source_target_pairs={{0,28},{1,5},{2,30},{3,7},{4,0},{5,9},{6,2},{7,11},{8,4},{9,13},{1... | collective-permute-start | bytes 393224 | tf_op jit(solution)/shard_map/ppermute | solution.py:40
  48.9 2.0 %collective-permute-start.18 = (f32[128,128]{1,0:T(8,128)S(1)}, f32[128,128]{1,0:T(8,128)S(1)}, u32[]{:S(2)}, u32[]{:S(2)}) collective-permute-start(f32[128,128]{1,0:T(8,128)S(1)} %get-tuple-element.53), channel_id=1, source_target_pairs={{0,8},{4,12},{8,16},{12,20},{16,24},{20,28},{24,0},{28,4},{1,9},{5... | collective-permute-start | bytes 196616 | tf_op jit(solution)/shard_map/ppermute | solution.py:15
  51.0 1.5 %collective-permute-done.15 = f32[256,128]{1,0:T(8,128)S(1)} collective-permute-done((f32[256,128]{1,0:T(8,128)S(1)}, f32[256,128]{1,0:T(8,128)S(1)}, u32[]{:S(2)}, u32[]{:S(2)}) %collective-permute-start.15) | collective-permute-done | bytes 131104 | tf_op jit(solution)/shard_map/ppermute | solution.py:40
  53.5 1.4 %collective-permute-done.18 = f32[128,128]{1,0:T(8,128)S(1)} collective-permute-done((f32[128,128]{1,0:T(8,128)S(1)}, f32[128,128]{1,0:T(8,128)S(1)}, u32[]{:S(2)}, u32[]{:S(2)}) %collective-permute-start.18) | collective-permute-done | bytes 65568 | tf_op jit(solution)/shard_map/ppermute | solution.py:15
  56.2 1.4 %collective-permute-start.21 = (f32[128,128]{1,0:T(8,128)S(1)}, f32[128,128]{1,0:T(8,128)S(1)}, u32[]{:S(2)}, u32[]{:S(2)}) collective-permute-start(f32[128,128]{1,0:T(8,128)S(1)} %get-tuple-element.37), channel_id=1, source_target_pairs={{0,3},{1,0},{2,1},{3,2},{4,7},{5,4},{6,5},{7,6},{8,11},{9,8},{10,9... | collective-permute-start | bytes 196616 | tf_op jit(solution)/shard_map/ppermute | solution.py:20
  58.8 1.3 %collective-permute-done.20.refs_2_ = f32[128,128]{1,0:T(8,128)S(1)} collective-permute-done((f32[128,128]{1,0:T(8,128)S(1)}, f32[128,128]{1,0:T(8,128)S(1)}, u32[]{:S(2)}, u32[]{:S(2)}) %collective-permute-start.20) | collective-permute-done | bytes 65568 | tf_op jit(solution)/shard_map/ppermute | solution.py:20
  64.5 1.4 %collective-permute-done.23 = f32[128,128]{1,0:T(8,128)S(1)} collective-permute-done((f32[128,128]{1,0:T(8,128)S(1)}, f32[128,128]{1,0:T(8,128)S(1)}, u32[]{:S(2)}, u32[]{:S(2)}) %collective-permute-start.23) | collective-permute-done | bytes 65568 | tf_op jit(solution)/shard_map/ppermute | solution.py:20
  66.0 1.4 %collective-permute-start.25 = (f32[128,128]{1,0:T(8,128)S(1)}, f32[128,128]{1,0:T(8,128)S(1)}, u32[]{:S(2)}, u32[]{:S(2)}) collective-permute-start(f32[128,128]{1,0:T(8,128)S(1)} %get-tuple-element.47), channel_id=1, source_target_pairs={{0,4},{4,8},{8,12},{12,16},{16,20},{20,24},{24,28},{28,0},{1,5},{5... | collective-permute-start | bytes 196616 | tf_op jit(solution)/shard_map/ppermute | solution.py:15
  67.4 3.4 %collective-permute-start.26 = (f32[128,128]{1,0:T(8,128)S(1)}, f32[128,128]{1,0:T(8,128)S(1)}, u32[]{:S(2)}, u32[]{:S(2)}) collective-permute-start(f32[128,128]{1,0:T(8,128)S(1)} %get-tuple-element.48), channel_id=1, source_target_pairs={{0,28},{4,0},{8,4},{12,8},{16,12},{20,16},{24,20},{28,24},{1,29},{... | collective-permute-start | bytes 196616 | tf_op jit(solution)/shard_map/ppermute | solution.py:15
  70.7 2.5 %collective-permute-done.25 = f32[128,128]{1,0:T(8,128)S(1)} collective-permute-done((f32[128,128]{1,0:T(8,128)S(1)}, f32[128,128]{1,0:T(8,128)S(1)}, u32[]{:S(2)}, u32[]{:S(2)}) %collective-permute-start.25) | collective-permute-done | bytes 65568 | tf_op jit(solution)/shard_map/ppermute | solution.py:15
  (54 shorter events, 20.6 us)
Async XLA Ops:
  0.9 10.4 %collective-permute-start = (f32[512,128]{1,0:T(8,128)S(1)}, f32[512,128]{1,0:T(8,128)S(1)}, u32[]{:S(2)}, u32[]{:S(2)}) collective-permute-start(f32[512,128]{1,0:T(8,128)S(1)} %convert_element_type.3.own), channel_id=1, source_target_pairs={{0,4},{1,29},{2,6},{3,31},{4,8},{5,1},{6,10},{7,3},{8,12},{9,5},{1... | collective-permute-start | bytes 786440 | tf_op jit(solution)/shard_map/ppermute | solution.py:151
  15.7 4.5 %collective-permute-start.3 = (f32[136,128]{1,0:T(8,128)S(1)}, f32[136,128]{1,0:T(8,128)S(1)}, u32[]{:S(2)}, u32[]{:S(2)}) collective-permute-start(f32[136,128]{1,0:T(8,128)S(1)} %get-tuple-element.27), channel_id=1, source_target_pairs={{0,2},{1,3},{2,0},{3,1},{4,6},{5,7},{6,4},{7,5},{8,10},{9,11},{10,... | collective-permute-start | bytes 208904 | tf_op jit(solution)/shard_map/ppermute | solution.py:20
  17.5 4.4 %collective-permute-start.2 = (f32[136,128]{1,0:T(8,128)S(1)}, f32[136,128]{1,0:T(8,128)S(1)}, u32[]{:S(2)}, u32[]{:S(2)}) collective-permute-start(f32[136,128]{1,0:T(8,128)S(1)} %get-tuple-element.26), channel_id=1, source_target_pairs={{0,1},{1,2},{2,3},{3,0},{4,5},{5,6},{6,7},{7,4},{8,9},{9,10},{10,1... | collective-permute-start | bytes 208904 | tf_op jit(solution)/shard_map/ppermute | solution.py:20
  22.1 7.8 %collective-permute-start.5 = (f32[256,128]{1,0:T(8,128)S(1)}, f32[256,128]{1,0:T(8,128)S(1)}, u32[]{:S(2)}, u32[]{:S(2)}) collective-permute-start(f32[256,128]{1,0:T(8,128)S(1)} %get-tuple-element.65), channel_id=1, source_target_pairs={{0,4},{1,29},{2,6},{3,31},{4,8},{5,1},{6,10},{7,3},{8,12},{9,5},{1... | collective-permute-start | bytes 393224 | tf_op jit(solution)/shard_map/ppermute | solution.py:40
  22.2 7.8 %collective-permute-start.6 = (f32[256,128]{1,0:T(8,128)S(1)}, f32[256,128]{1,0:T(8,128)S(1)}, u32[]{:S(2)}, u32[]{:S(2)}) collective-permute-start(f32[256,128]{1,0:T(8,128)S(1)} %get-tuple-element.64), channel_id=1, source_target_pairs={{0,28},{1,5},{2,30},{3,7},{4,0},{5,9},{6,2},{7,11},{8,4},{9,13},{1... | collective-permute-start | bytes 393224 | tf_op jit(solution)/shard_map/ppermute | solution.py:40
  26.9 4.5 %collective-permute-start.7 = (f32[128,128]{1,0:T(8,128)S(1)}, f32[128,128]{1,0:T(8,128)S(1)}, u32[]{:S(2)}, u32[]{:S(2)}) collective-permute-start(f32[128,128]{1,0:T(8,128)S(1)} %select_add_fusion.5), channel_id=1, source_target_pairs={{0,24},{4,28},{8,0},{12,4},{16,8},{20,12},{24,16},{28,20},{1,25},{... | collective-permute-start | bytes 196616 | tf_op jit(solution)/shard_map/ppermute | solution.py:15
  26.9 6.1 %collective-permute-start.8 = (f32[128,128]{1,0:T(8,128)S(1)}, f32[128,128]{1,0:T(8,128)S(1)}, u32[]{:S(2)}, u32[]{:S(2)}) collective-permute-start(f32[128,128]{1,0:T(8,128)S(1)} %get-tuple-element.46), channel_id=1, source_target_pairs={{0,8},{4,12},{8,16},{12,20},{16,24},{20,28},{24,0},{28,4},{1,9},{5... | collective-permute-start | bytes 196616 | tf_op jit(solution)/shard_map/ppermute | solution.py:15
  33.0 4.3 %collective-permute-start.10 = (f32[128,128]{1,0:T(8,128)S(1)}, f32[128,128]{1,0:T(8,128)S(1)}, u32[]{:S(2)}, u32[]{:S(2)}) collective-permute-start(f32[128,128]{1,0:T(8,128)S(1)} %get-tuple-element.61), channel_id=1, source_target_pairs={{0,2},{1,3},{2,0},{3,1},{4,6},{5,7},{6,4},{7,5},{8,10},{9,11},{10,... | collective-permute-start | bytes 196616 | tf_op jit(solution)/shard_map/ppermute | solution.py:20
  34.3 3.7 %collective-permute-start.9 = (f32[128,128]{1,0:T(8,128)S(1)}, f32[128,128]{1,0:T(8,128)S(1)}, u32[]{:S(2)}, u32[]{:S(2)}) collective-permute-start(f32[128,128]{1,0:T(8,128)S(1)} %get-tuple-element.62), channel_id=1, source_target_pairs={{0,1},{1,2},{2,3},{3,0},{4,5},{5,6},{6,7},{7,4},{8,9},{9,10},{10,1... | collective-permute-start | bytes 196616 | tf_op jit(solution)/shard_map/ppermute | solution.py:20
  34.3 3.7 %collective-permute-start.11 = (f32[128,128]{1,0:T(8,128)S(1)}, f32[128,128]{1,0:T(8,128)S(1)}, u32[]{:S(2)}, u32[]{:S(2)}) collective-permute-start(f32[128,128]{1,0:T(8,128)S(1)} %get-tuple-element.41), channel_id=1, source_target_pairs={{0,3},{1,0},{2,1},{3,2},{4,7},{5,4},{6,5},{7,6},{8,11},{9,8},{10,9... | collective-permute-start | bytes 196616 | tf_op jit(solution)/shard_map/ppermute | solution.py:20
  38.6 3.7 %collective-permute-start.12 = (f32[128,128]{1,0:T(8,128)S(1)}, f32[128,128]{1,0:T(8,128)S(1)}, u32[]{:S(2)}, u32[]{:S(2)}) collective-permute-start(f32[128,128]{1,0:T(8,128)S(1)} %get-tuple-element.30), channel_id=1, source_target_pairs={{0,1},{1,2},{2,3},{3,0},{4,5},{5,6},{6,7},{7,4},{8,9},{9,10},{10,1... | collective-permute-start | bytes 196616 | tf_op jit(solution)/shard_map/ppermute | solution.py:20
  39.5 4.5 %collective-permute-start.13 = (f32[128,128]{1,0:T(8,128)S(1)}, f32[128,128]{1,0:T(8,128)S(1)}, u32[]{:S(2)}, u32[]{:S(2)}) collective-permute-start(f32[128,128]{1,0:T(8,128)S(1)} %get-tuple-element.31), channel_id=1, source_target_pairs={{0,2},{1,3},{2,0},{3,1},{4,6},{5,7},{6,4},{7,5},{8,10},{9,11},{10,... | collective-permute-start | bytes 196616 | tf_op jit(solution)/shard_map/ppermute | solution.py:20
  44.1 8.3 %collective-permute-start.15 = (f32[256,128]{1,0:T(8,128)S(1)}, f32[256,128]{1,0:T(8,128)S(1)}, u32[]{:S(2)}, u32[]{:S(2)}) collective-permute-start(f32[256,128]{1,0:T(8,128)S(1)} %get-tuple-element.60), channel_id=1, source_target_pairs={{0,4},{1,29},{2,6},{3,31},{4,8},{5,1},{6,10},{7,3},{8,12},{9,5},{1... | collective-permute-start | bytes 393224 | tf_op jit(solution)/shard_map/ppermute | solution.py:40
  45.4 7.0 %collective-permute-start.16 = (f32[256,128]{1,0:T(8,128)S(1)}, f32[256,128]{1,0:T(8,128)S(1)}, u32[]{:S(2)}, u32[]{:S(2)}) collective-permute-start(f32[256,128]{1,0:T(8,128)S(1)} %get-tuple-element.59), channel_id=1, source_target_pairs={{0,28},{1,5},{2,30},{3,7},{4,0},{5,9},{6,2},{7,11},{8,4},{9,13},{1... | collective-permute-start | bytes 393224 | tf_op jit(solution)/shard_map/ppermute | solution.py:40
  48.9 4.6 %collective-permute-start.17 = (f32[128,128]{1,0:T(8,128)S(1)}, f32[128,128]{1,0:T(8,128)S(1)}, u32[]{:S(2)}, u32[]{:S(2)}) collective-permute-start(f32[128,128]{1,0:T(8,128)S(1)} %get-tuple-element.52), channel_id=1, source_target_pairs={{0,24},{4,28},{8,0},{12,4},{16,8},{20,12},{24,16},{28,20},{1,25},{... | collective-permute-start | bytes 196616 | tf_op jit(solution)/shard_map/ppermute | solution.py:15
  48.9 6.1 %collective-permute-start.18 = (f32[128,128]{1,0:T(8,128)S(1)}, f32[128,128]{1,0:T(8,128)S(1)}, u32[]{:S(2)}, u32[]{:S(2)}) collective-permute-start(f32[128,128]{1,0:T(8,128)S(1)} %get-tuple-element.53), channel_id=1, source_target_pairs={{0,8},{4,12},{8,16},{12,20},{16,24},{20,28},{24,0},{28,4},{1,9},{5... | collective-permute-start | bytes 196616 | tf_op jit(solution)/shard_map/ppermute | solution.py:15
  55.1 3.8 %collective-permute-start.19 = (f32[128,128]{1,0:T(8,128)S(1)}, f32[128,128]{1,0:T(8,128)S(1)}, u32[]{:S(2)}, u32[]{:S(2)}) collective-permute-start(f32[128,128]{1,0:T(8,128)S(1)} %get-tuple-element.57), channel_id=1, source_target_pairs={{0,1},{1,2},{2,3},{3,0},{4,5},{5,6},{6,7},{7,4},{8,9},{9,10},{10,1... | collective-permute-start | bytes 196616 | tf_op jit(solution)/shard_map/ppermute | solution.py:20
  55.1 5.0 %collective-permute-start.20 = (f32[128,128]{1,0:T(8,128)S(1)}, f32[128,128]{1,0:T(8,128)S(1)}, u32[]{:S(2)}, u32[]{:S(2)}) collective-permute-start(f32[128,128]{1,0:T(8,128)S(1)} %get-tuple-element.56), channel_id=1, source_target_pairs={{0,2},{1,3},{2,0},{3,1},{4,6},{5,7},{6,4},{7,5},{8,10},{9,11},{10,... | collective-permute-start | bytes 196616 | tf_op jit(solution)/shard_map/ppermute | solution.py:20
  56.2 4.0 %collective-permute-start.21 = (f32[128,128]{1,0:T(8,128)S(1)}, f32[128,128]{1,0:T(8,128)S(1)}, u32[]{:S(2)}, u32[]{:S(2)}) collective-permute-start(f32[128,128]{1,0:T(8,128)S(1)} %get-tuple-element.37), channel_id=1, source_target_pairs={{0,3},{1,0},{2,1},{3,2},{4,7},{5,4},{6,5},{7,6},{8,11},{9,8},{10,9... | collective-permute-start | bytes 196616 | tf_op jit(solution)/shard_map/ppermute | solution.py:20
  60.7 3.7 %collective-permute-start.22 = (f32[128,128]{1,0:T(8,128)S(1)}, f32[128,128]{1,0:T(8,128)S(1)}, u32[]{:S(2)}, u32[]{:S(2)}) collective-permute-start(f32[128,128]{1,0:T(8,128)S(1)} %get-tuple-element.34), channel_id=1, source_target_pairs={{0,1},{1,2},{2,3},{3,0},{4,5},{5,6},{6,7},{7,4},{8,9},{9,10},{10,1... | collective-permute-start | bytes 196616 | tf_op jit(solution)/shard_map/ppermute | solution.py:20
  61.4 4.6 %collective-permute-start.23 = (f32[128,128]{1,0:T(8,128)S(1)}, f32[128,128]{1,0:T(8,128)S(1)}, u32[]{:S(2)}, u32[]{:S(2)}) collective-permute-start(f32[128,128]{1,0:T(8,128)S(1)} %get-tuple-element.35), channel_id=1, source_target_pairs={{0,2},{1,3},{2,0},{3,1},{4,6},{5,7},{6,4},{7,5},{8,10},{9,11},{10,... | collective-permute-start | bytes 196616 | tf_op jit(solution)/shard_map/ppermute | solution.py:20
  62.4 3.5 %collective-permute-start.24 = (f32[128,128]{1,0:T(8,128)S(1)}, f32[128,128]{1,0:T(8,128)S(1)}, u32[]{:S(2)}, u32[]{:S(2)}) collective-permute-start(f32[128,128]{1,0:T(8,128)S(1)} %get-tuple-element.36), channel_id=1, source_target_pairs={{0,3},{1,0},{2,1},{3,2},{4,7},{5,4},{6,5},{7,6},{8,11},{9,8},{10,9... | collective-permute-start | bytes 196616 | tf_op jit(solution)/shard_map/ppermute | solution.py:20
  66.0 7.3 %collective-permute-start.25 = (f32[128,128]{1,0:T(8,128)S(1)}, f32[128,128]{1,0:T(8,128)S(1)}, u32[]{:S(2)}, u32[]{:S(2)}) collective-permute-start(f32[128,128]{1,0:T(8,128)S(1)} %get-tuple-element.47), channel_id=1, source_target_pairs={{0,4},{4,8},{8,12},{12,16},{16,20},{20,24},{24,28},{28,0},{1,5},{5... | collective-permute-start | bytes 196616 | tf_op jit(solution)/shard_map/ppermute | solution.py:15
  67.4 5.9 %collective-permute-start.26 = (f32[128,128]{1,0:T(8,128)S(1)}, f32[128,128]{1,0:T(8,128)S(1)}, u32[]{:S(2)}, u32[]{:S(2)}) collective-permute-start(f32[128,128]{1,0:T(8,128)S(1)} %get-tuple-element.48), channel_id=1, source_target_pairs={{0,28},{4,0},{8,4},{12,8},{16,12},{20,16},{24,20},{28,24},{1,29},{... | collective-permute-start | bytes 196616 | tf_op jit(solution)/shard_map/ppermute | solution.py:15
  (4 other events, 24.5 us)
